TPU v7x, 32 devices: a whole 2x2x4 slice. The times are simulated.
32 devices in a mesh: rep: 8 (over z, y), shard: 4 (over x, core).
Axes of the slice: x: 2, y: 2, z: 4, core: 2. Of those that a mesh axis runs over, the one named last changes fastest.
Arguments:
- hidden_in: bfloat16 [32768, 768], P(('rep', 'shard')), may hold values from -6 to 6
- mask_ids: int32 [32768], P(('rep', 'shard')), may hold values 0 or 1
- time_ids: int32 [16, 9], replicated, may hold values from 0 to 999
- time_table: float32 [1000, 128], replicated, may hold values from -6 to 6
- w_qkv: bfloat16 [768, 2304], P('shard'), may hold values from -0.21875 to 0.21875
- w_proj: bfloat16 [768, 768], P('shard'), may hold values from -6 to 6
- w_up: bfloat16 [768, 3072], P('shard'), may hold values from -0.21875 to 0.21875
- w_down: bfloat16 [3072, 768], P('shard'), may hold values from -0.109375 to 0.109375
- w_ada: bfloat16 [128, 4608], P('shard'), may hold values from -0.5 to 0.5
- gain_attn: bfloat16 [768], P('shard'), may hold values from 0.25 to 1.75
- gain_mlp: bfloat16 [768], P('shard'), may hold values from 0.25 to 1.75
- bias_up: bfloat16 [3072], P('shard'), may hold values from -3 to 3
- bias_down: bfloat16 [768], P('shard'), may hold values from -3 to 3
- bias_ada: bfloat16 [4608], P('shard'), may hold values from -3 to 3
- mask_embed: bfloat16 [768], P('shard'), may hold values from -6 to 6
- cotangent: bfloat16 [32768, 768], P(('rep', 'shard')), may hold values from -6 to 6
Outputs:
- block_out: bfloat16 [32768, 768], P(('rep', 'shard'))
- grad_hidden: float32 [32768, 768], P(('rep', 'shard'))
- grad_time: float32 [1000, 128], replicated
- grad_qkv: float32 [768, 2304], P('shard')
- grad_proj: float32 [768, 768], P('shard')
- grad_up: float32 [768, 3072], P('shard')
- grad_down: float32 [3072, 768], P('shard')
- grad_ada: float32 [128, 4608], P('shard')
- grad_gain_attn: float32 [768], P('shard')
- grad_gain_mlp: float32 [768], P('shard')
- grad_bias_up: float32 [3072], P('shard')
- grad_bias_down: float32 [768], P('shard')
- grad_bias_ada: float32 [4608], P('shard')
- grad_mask_embed: float32 [768], P('shard')
All inputs are finite; a program needn't handle non-finite values. No bound on the sum of `mask_ids` on one device may be relied on, other than what follows from the above.
Results may differ from a plain program's by a relative error of at most 0.0085.
The roundings to bfloat16 on the way count: a program that leaves them out, or rounds other values in their place, can miss the bound.
Values may be sent and summed in bfloat16 or wider, within the bound.
No kernel may reach another device: no remote copies, remote signals or barrier semaphores. Data moves between devices by JAX's collectives and lax.ppermute only.
A program may use at most 192 MiB of HBM per device.

v0:
```python
from functools import partial

import jax
import jax.numpy as jnp
from jax import lax
from jax.sharding import PartitionSpec as P

D = 768
HEADS = 12
HDIM = 64
STEPS = 1000
CLEN = 128
CONTS = 8
PROMPT = 1024


eps_norm = 1e-06
neg_large = -1e30


def partner(value, axis, apart):
    mask = 2**apart
    pairs = [(source, source ^ mask) for source in range(lax.axis_size(axis))]
    return lax.ppermute(value, axis, pairs)


def layer_norm(values):
    mean_value = jnp.mean(values, -1, keepdims=True)
    centered = values - mean_value
    inv_std = lax.rsqrt(jnp.mean(centered * centered, -1, keepdims=True) + eps_norm)
    return (centered * inv_std, inv_std)


def norm_back(gradient, normed, inv_std):
    return inv_std * (
        gradient
        - jnp.mean(gradient, -1, keepdims=True)
        - normed * jnp.mean(gradient * normed, -1, keepdims=True)
    )


def rotary(values, cosine, sine_val):
    half_dim = values.shape[-1] // 2
    first_half = values[..., :half_dim]
    second = values[..., half_dim:]
    return jnp.concatenate(
        [first_half * cosine - second * sine_val, first_half * sine_val + second * cosine], -1
    )


def product(left_mat, right_mat):
    return jnp.dot(left_mat, right_mat, preferred_element_type=jnp.float32)


def times_trans(left_mat, right_mat):
    return lax.dot_general(
        left_mat, right_mat, (((1,), (1,)), ((), ())), preferred_element_type=jnp.float32
    )


def contract(left_mat, right_mat):
    return lax.dot_general(
        left_mat, right_mat, (((0,), (0,)), ((), ())), preferred_element_type=jnp.float32
    )


def split_heads(values):
    groups = values.shape[0] // PROMPT
    return values.reshape(groups, PROMPT, HEADS, HDIM).transpose(2, 0, 1, 3)


def merge_heads(values):
    groups = values.shape[1]
    return values.transpose(1, 2, 0, 3).reshape(groups * PROMPT, HEADS * HDIM)


def blocks(values):
    return values.reshape(values.shape[0], CONTS, CLEN, HDIM)


def own_allowed():
    return (jnp.arange(CONTS, dtype=jnp.int32) >= CONTS // 2)[None, :, None, None]


def head_forward(operands):
    queries, key_main, value_main, key_own, value_own = operands
    scaling = HDIM ** (-0.5)
    query_blk = blocks(queries)
    score_main = (
        jnp.einsum("gcqd,gkd->gcqk", query_blk, key_main, preferred_element_type=jnp.float32)
        * scaling
    )
    score_own = (
        jnp.einsum(
            "gcqd,gckd->gcqk", query_blk, blocks(key_own), preferred_element_type=jnp.float32
        )
        * scaling
    )
    score_own = jnp.where(own_allowed(), score_own, neg_large)
    row_max = jnp.maximum(jnp.max(score_main, -1), jnp.max(score_own, -1))
    denom_sum = jnp.sum(jnp.exp(score_main - row_max[..., None]), -1) + jnp.sum(
        jnp.exp(score_own - row_max[..., None]), -1
    )
    log_sum = row_max + jnp.log(denom_sum)
    prob_main = jnp.exp(score_main - log_sum[..., None]).astype(jnp.bfloat16)
    prob_own = jnp.exp(score_own - log_sum[..., None]).astype(jnp.bfloat16)
    output = jnp.einsum("gcqk,gkd->gcqd", prob_main, value_main, preferred_element_type=jnp.float32)
    output = output + jnp.einsum(
        "gcqk,gckd->gcqd", prob_own, blocks(value_own), preferred_element_type=jnp.float32
    )
    return (output.reshape(queries.shape[0], PROMPT, HDIM), log_sum)


def head_backward(operands):
    queries, key_main, value_main, key_own, value_own, log_sum, grad_out = operands
    scaling = HDIM ** (-0.5)
    groups = queries.shape[0]
    query_blk = blocks(queries)
    grad_blk = blocks(grad_out)
    key_blk = blocks(key_own)
    score_main = (
        jnp.einsum("gcqd,gkd->gcqk", query_blk, key_main, preferred_element_type=jnp.float32)
        * scaling
    )
    prob_main = jnp.exp(score_main - log_sum[..., None])
    score_own = (
        jnp.einsum("gcqd,gckd->gcqk", query_blk, key_blk, preferred_element_type=jnp.float32)
        * scaling
    )
    score_own = jnp.where(own_allowed(), score_own, neg_large)
    prob_own = jnp.exp(score_own - log_sum[..., None])
    grad_prob_main = jnp.einsum(
        "gcqd,gkd->gcqk", grad_blk, value_main, preferred_element_type=jnp.float32
    )
    grad_prob_own = jnp.einsum(
        "gcqd,gckd->gcqk", grad_blk, blocks(value_own), preferred_element_type=jnp.float32
    )
    row_dot = jnp.sum(grad_prob_main * prob_main, -1) + jnp.sum(grad_prob_own * prob_own, -1)
    grad_value_main = jnp.einsum(
        "gcqk,gcqd->gkd",
        prob_main.astype(jnp.bfloat16),
        grad_blk,
        preferred_element_type=jnp.float32,
    )
    grad_value_own = jnp.einsum(
        "gcqk,gcqd->gckd",
        prob_own.astype(jnp.bfloat16),
        grad_blk,
        preferred_element_type=jnp.float32,
    ).reshape(groups, PROMPT, HDIM)
    grad_score_main = (prob_main * (grad_prob_main - row_dot[..., None])).astype(jnp.bfloat16)
    grad_score_own = (prob_own * (grad_prob_own - row_dot[..., None])).astype(jnp.bfloat16)
    grad_query = jnp.einsum(
        "gcqk,gkd->gcqd", grad_score_main, key_main, preferred_element_type=jnp.float32
    )
    grad_query = grad_query + jnp.einsum(
        "gcqk,gckd->gcqd", grad_score_own, key_blk, preferred_element_type=jnp.float32
    )
    grad_key_main = (
        jnp.einsum("gcqk,gcqd->gkd", grad_score_main, query_blk, preferred_element_type=jnp.float32)
        * scaling
    )
    grad_key_own = (
        jnp.einsum(
            "gcqk,gcqd->gckd", grad_score_own, query_blk, preferred_element_type=jnp.float32
        ).reshape(groups, PROMPT, HDIM)
        * scaling
    )
    return (
        (grad_query * scaling).reshape(groups, PROMPT, HDIM),
        grad_key_main,
        grad_value_main,
        grad_key_own,
        grad_value_own,
    )


def on_device(
    hidden_in,
    mask_ids,
    time_ids,
    time_table,
    w_qkv,
    w_proj,
    w_up,
    w_down,
    w_ada,
    gain_attn,
    gain_mlp,
    bias_up,
    bias_down,
    bias_ada,
    mask_embed,
    cotangent,
):
    sharded = (
        w_qkv,
        w_proj,
        w_up,
        w_down,
        w_ada,
        gain_attn,
        gain_mlp,
        bias_up,
        bias_down,
        bias_ada,
        mask_embed,
    )
    gathered = (
        lax.all_gather(sharded[0], "shard", axis=0, tiled=True),
        lax.all_gather(sharded[1], "shard", axis=0, tiled=True),
        lax.all_gather(sharded[2], "shard", axis=0, tiled=True),
        lax.all_gather(sharded[3], "shard", axis=0, tiled=True),
        lax.all_gather(sharded[4], "shard", axis=0, tiled=True),
        lax.all_gather(sharded[5], "shard", axis=0, tiled=True),
        lax.all_gather(sharded[6], "shard", axis=0, tiled=True),
        lax.all_gather(sharded[7], "shard", axis=0, tiled=True),
        lax.all_gather(sharded[8], "shard", axis=0, tiled=True),
        lax.all_gather(sharded[9], "shard", axis=0, tiled=True),
        lax.all_gather(sharded[10], "shard", axis=0, tiled=True),
    )
    (
        qkv_mat,
        proj_mat,
        up_mat,
        down_mat,
        ada_mat,
        attn_gain,
        mlp_gain,
        up_bias,
        down_bias,
        ada_bias,
        embed_vec,
    ) = gathered
    shard_index = lax.axis_index("shard")
    rep_index = lax.axis_index("rep")
    half_index = shard_index % 2
    is_first = half_index == 0
    pair_index = (rep_index * lax.axis_size("shard") + shard_index) // 2
    tok_count = hidden_in.shape[0]
    groups = tok_count // PROMPT
    half_len = PROMPT // 2
    shape_four = (groups, CONTS, CLEN, D)
    my_times = lax.dynamic_slice_in_dim(time_ids, pair_index * groups, groups, 0).reshape(-1)
    one_hot = (my_times[:, None] == jnp.arange(STEPS, dtype=jnp.int32)[None, :]).astype(jnp.float32)
    cond = jnp.dot(one_hot, time_table, precision=lax.Precision.HIGHEST)
    silu_value, silu_back = jax.vjp(jax.nn.silu, cond)
    silu_low = silu_value.astype(jnp.bfloat16)
    modul = (product(silu_low, ada_mat) + ada_bias.astype(jnp.float32)).reshape(
        groups, CONTS + 1, 6 * D
    )
    block_ids = jnp.arange(CONTS, dtype=jnp.int32)
    seg_index = jnp.where(
        block_ids < CONTS // 2, 0, 1 + half_index * (CONTS // 2) + block_ids - CONTS // 2
    )
    select = (seg_index[:, None] == jnp.arange(CONTS + 1, dtype=jnp.int32)[None, :]).astype(
        jnp.float32
    )
    tok_mod = jnp.einsum("bs,gsf->gbf", select, modul, precision=lax.Precision.HIGHEST)
    shift_attn, scale_attn, gate_attn, shift_mlp, scale_mlp, gate_mlp = jnp.split(
        tok_mod[:, :, None, :], 6, axis=3
    )
    masked = (mask_ids == 1).reshape(groups, CONTS, CLEN, 1)
    start = jnp.where(
        masked, embed_vec.astype(jnp.float32), hidden_in.astype(jnp.float32).reshape(shape_four)
    )
    normed_attn, inv_attn = layer_norm(start)
    attn_gain_f = attn_gain.astype(jnp.float32)
    attn_input = (
        (normed_attn * attn_gain_f * (1.0 + scale_attn) + shift_attn)
        .astype(jnp.bfloat16)
        .reshape(tok_count, D)
    )
    qkv = product(attn_input, qkv_mat)
    local_ids = jnp.arange(tok_count, dtype=jnp.int32) % PROMPT
    positions = jnp.where(
        local_ids // CLEN < CONTS // 2, half_index * half_len + local_ids, PROMPT + local_ids % CLEN
    ).astype(jnp.float32)
    freqs = 10000.0 ** (-(2.0 * jnp.arange(HDIM // 2, dtype=jnp.float32)) / HDIM)
    angles = positions[:, None] * freqs[None, :]
    cosine = jnp.cos(angles)[:, None, :]
    sine_val = jnp.sin(angles)[:, None, :]
    queries = (
        rotary(qkv[:, :D].reshape(tok_count, HEADS, HDIM), cosine, sine_val)
        .astype(jnp.bfloat16)
        .reshape(tok_count, D)
    )
    keys_low = (
        rotary(qkv[:, D : 2 * D].reshape(tok_count, HEADS, HDIM), cosine, sine_val)
        .astype(jnp.bfloat16)
        .reshape(tok_count, D)
    )
    values_low = qkv[:, 2 * D :].astype(jnp.bfloat16)
    own_keys = keys_low.reshape(groups, PROMPT, D)[:, :half_len]
    own_values = values_low.reshape(groups, PROMPT, D)[:, :half_len]
    received = partner((own_keys, own_values), "shard", 0)
    key_main = jnp.where(
        is_first,
        jnp.concatenate([own_keys, received[0]], 1),
        jnp.concatenate([received[0], own_keys], 1),
    ).reshape(tok_count, D)
    value_main = jnp.where(
        is_first,
        jnp.concatenate([own_values, received[1]], 1),
        jnp.concatenate([received[1], own_values], 1),
    ).reshape(tok_count, D)
    operands = (
        split_heads(queries),
        split_heads(key_main),
        split_heads(value_main),
        split_heads(keys_low),
        split_heads(values_low),
    )
    attn_out, log_sum = lax.map(head_forward, operands)
    attn_low = merge_heads(attn_out).astype(jnp.bfloat16)
    attn_proj = product(attn_low, proj_mat).reshape(shape_four)
    middle = start + gate_attn * attn_proj
    normed_mlp, inv_mlp = layer_norm(middle)
    mlp_gain_f = mlp_gain.astype(jnp.float32)
    mlp_input = (
        (normed_mlp * mlp_gain_f * (1.0 + scale_mlp) + shift_mlp)
        .astype(jnp.bfloat16)
        .reshape(tok_count, D)
    )
    pre_act = product(mlp_input, up_mat) + up_bias.astype(jnp.float32)
    act_value, gelu_back = jax.vjp(partial(jax.nn.gelu, approximate=True), pre_act)
    act_low = act_value.astype(jnp.bfloat16)
    mlp_out = (product(act_low, down_mat) + down_bias.astype(jnp.float32)).reshape(shape_four)
    block_out = (middle + gate_mlp * mlp_out).astype(jnp.bfloat16).reshape(tok_count, D)
    back_weights = (
        lax.all_gather(sharded[0], "shard", axis=0, tiled=True),
        lax.all_gather(sharded[1], "shard", axis=0, tiled=True),
        lax.all_gather(sharded[2], "shard", axis=0, tiled=True),
        lax.all_gather(sharded[3], "shard", axis=0, tiled=True),
        lax.all_gather(sharded[4], "shard", axis=0, tiled=True),
        lax.all_gather(sharded[5], "shard", axis=0, tiled=True),
        lax.all_gather(sharded[6], "shard", axis=0, tiled=True),
        lax.all_gather(sharded[7], "shard", axis=0, tiled=True),
        lax.all_gather(sharded[8], "shard", axis=0, tiled=True),
        lax.all_gather(sharded[9], "shard", axis=0, tiled=True),
        lax.all_gather(sharded[10], "shard", axis=0, tiled=True),
    )
    qkv_back, proj_back, up_back, down_back, ada_back = back_weights[:5]
    grad_top = cotangent.astype(jnp.float32).reshape(shape_four)
    grad_gate_mlp = jnp.sum(grad_top * mlp_out, 2)
    grad_branch = (gate_mlp * grad_top).astype(jnp.bfloat16).reshape(tok_count, D)
    grad_down = contract(act_low, grad_branch)
    grad_bias_down = jnp.sum(grad_branch.astype(jnp.float32), 0)
    grad_act = times_trans(grad_branch, down_back)
    grad_pre = gelu_back(grad_act)[0].astype(jnp.bfloat16)
    grad_up = contract(mlp_input, grad_pre)
    grad_bias_up = jnp.sum(grad_pre.astype(jnp.float32), 0)
    grad_n_two = times_trans(grad_pre, up_back).reshape(shape_four)
    grad_shift_mlp = jnp.sum(grad_n_two, 2)
    grad_scale_mlp = jnp.sum(grad_n_two * normed_mlp * mlp_gain_f, 2)
    grad_affine_mlp = grad_n_two * (1.0 + scale_mlp)
    grad_gain_mlp = jnp.sum(grad_affine_mlp * normed_mlp, (0, 1, 2))
    grad_middle = grad_top + norm_back(grad_affine_mlp * mlp_gain_f, normed_mlp, inv_mlp)
    grad_gate_attn = jnp.sum(grad_middle * attn_proj, 2)
    grad_att = (gate_attn * grad_middle).astype(jnp.bfloat16).reshape(tok_count, D)
    grad_proj = contract(attn_low, grad_att)
    grad_attn_o = times_trans(grad_att, proj_back).astype(jnp.bfloat16)
    back_ops = operands + (log_sum, split_heads(grad_attn_o))
    grad_queries, grad_key_main, grad_value_main, grad_key_own, grad_value_own = lax.map(
        head_backward, back_ops
    )
    key_main_grp = merge_heads(grad_key_main).reshape(groups, PROMPT, D)
    value_main_grp = merge_heads(grad_value_main).reshape(groups, PROMPT, D)
    mine_keys = jnp.where(is_first, key_main_grp[:, :half_len], key_main_grp[:, half_len:])
    other_keys = jnp.where(is_first, key_main_grp[:, half_len:], key_main_grp[:, :half_len])
    mine_values = jnp.where(is_first, value_main_grp[:, :half_len], value_main_grp[:, half_len:])
    other_values = jnp.where(is_first, value_main_grp[:, half_len:], value_main_grp[:, :half_len])
    returned = partner((other_keys, other_values), "shard", 0)
    zero_half = jnp.zeros((groups, half_len, D), jnp.float32)
    grad_keys = jnp.concatenate([mine_keys + returned[0], zero_half], 1).reshape(
        tok_count, D
    ) + merge_heads(grad_key_own)
    grad_values = jnp.concatenate([mine_values + returned[1], zero_half], 1).reshape(
        tok_count, D
    ) + merge_heads(grad_value_own)
    query_raw = rotary(
        merge_heads(grad_queries).reshape(tok_count, HEADS, HDIM), cosine, -sine_val
    ).reshape(tok_count, D)
    key_raw = rotary(grad_keys.reshape(tok_count, HEADS, HDIM), cosine, -sine_val).reshape(
        tok_count, D
    )
    grad_qkv_low = jnp.concatenate([query_raw, key_raw, grad_values], 1).astype(jnp.bfloat16)
    grad_qkv = contract(attn_input, grad_qkv_low)
    grad_n_one = times_trans(grad_qkv_low, qkv_back).reshape(shape_four)
    grad_shift_attn = jnp.sum(grad_n_one, 2)
    grad_scale_attn = jnp.sum(grad_n_one * normed_attn * attn_gain_f, 2)
    grad_affine_attn = grad_n_one * (1.0 + scale_attn)
    grad_gain_attn = jnp.sum(grad_affine_attn * normed_attn, (0, 1, 2))
    grad_start = grad_middle + norm_back(grad_affine_attn * attn_gain_f, normed_attn, inv_attn)
    grad_hidden = jnp.where(masked, 0.0, grad_start).reshape(tok_count, D)
    grad_mask_embed = jnp.sum(jnp.where(masked, grad_start, 0.0), (0, 1, 2))
    grad_mod = jnp.concatenate(
        [
            grad_shift_attn,
            grad_scale_attn,
            grad_gate_attn,
            grad_shift_mlp,
            grad_scale_mlp,
            grad_gate_mlp,
        ],
        -1,
    )
    grad_seg = jnp.einsum("bs,gbf->gsf", select, grad_mod, precision=lax.Precision.HIGHEST).reshape(
        groups * (CONTS + 1), 6 * D
    )
    grad_ada = lax.dot_general(
        silu_low.astype(jnp.float32),
        grad_seg,
        (((0,), (0,)), ((), ())),
        precision=lax.Precision.HIGHEST,
    )
    grad_bias_ada = jnp.sum(grad_seg, 0)
    grad_silu = lax.dot_general(
        grad_seg,
        ada_back.astype(jnp.float32),
        (((1,), (1,)), ((), ())),
        precision=lax.Precision.HIGHEST,
    )
    grad_cond = silu_back(grad_silu)[0]
    table_term = lax.dot_general(
        one_hot, grad_cond, (((0,), (0,)), ((), ())), precision=lax.Precision.HIGHEST
    )
    grad_time = lax.psum(table_term, ("rep", "shard"))
    grads = (
        grad_qkv,
        grad_proj,
        grad_up,
        grad_down,
        grad_ada,
        grad_gain_attn,
        grad_gain_mlp,
        grad_bias_up,
        grad_bias_down,
        grad_bias_ada,
        grad_mask_embed,
    )
    shares = (
        lax.psum_scatter(grads[0], "shard", scatter_dimension=0, tiled=True),
        lax.psum_scatter(grads[1], "shard", scatter_dimension=0, tiled=True),
        lax.psum_scatter(grads[2], "shard", scatter_dimension=0, tiled=True),
        lax.psum_scatter(grads[3], "shard", scatter_dimension=0, tiled=True),
        lax.psum_scatter(grads[4], "shard", scatter_dimension=0, tiled=True),
        lax.psum_scatter(grads[5], "shard", scatter_dimension=0, tiled=True),
        lax.psum_scatter(grads[6], "shard", scatter_dimension=0, tiled=True),
        lax.psum_scatter(grads[7], "shard", scatter_dimension=0, tiled=True),
        lax.psum_scatter(grads[8], "shard", scatter_dimension=0, tiled=True),
        lax.psum_scatter(grads[9], "shard", scatter_dimension=0, tiled=True),
        lax.psum_scatter(grads[10], "shard", scatter_dimension=0, tiled=True),
    )
    summed = lax.psum(
        (
            shares[0],
            shares[1],
            shares[2],
            shares[3],
            shares[4],
            shares[5],
            shares[6],
            shares[7],
            shares[8],
            shares[9],
            shares[10],
        ),
        "rep",
    )
    return (block_out, grad_hidden, grad_time) + tuple(summed)


def solution(mesh):
    in_specs = (
        P(("rep", "shard"), None),
        P(("rep", "shard")),
        P(),
        P(),
        P("shard", None),
        P("shard", None),
        P("shard", None),
        P("shard", None),
        P("shard", None),
        P("shard"),
        P("shard"),
        P("shard"),
        P("shard"),
        P("shard"),
        P("shard"),
        P(("rep", "shard"), None),
    )
    out_specs = (
        P(("rep", "shard"), None),
        P(("rep", "shard"), None),
        P(),
        P("shard", None),
        P("shard", None),
        P("shard", None),
        P("shard", None),
        P("shard", None),
        P("shard"),
        P("shard"),
        P("shard"),
        P("shard"),
        P("shard"),
        P("shard"),
    )
    return jax.shard_map(
        on_device, mesh=mesh, in_specs=in_specs, out_specs=out_specs, check_vma=False
    )
```

profile of v0, /device:TPU:10, one launch (start us, length us, event | category | flops | bytes accessed | tf_op | source)
XLA Modules:
  0.0 1177.1 jit_solution(14522430534345859399)
XLA Ops:
  15.4 6.1 all-reduce.15
  22.2 5.2 all-gather
  35.0 2.2 fusion.70
  37.2 22.7 %all-gather.10.cloned.1.call-done = bf16[768,2304]{1,0:T(8,128)(2,1)} async-done(((bf16[192,2304]{1,0:T(8,128)(2,1)}), bf16[768,2304]{1,0:T(8,128)(2,1)}) %all-gather.10.cloned.1.call-update) | async-done | bytes 3538960 | tf_op jit(solution)/shard_map/all_gather | solution.py:210
  59.9 6.3 fusion.133
  67.8 3.7 fusion.130
  72.1 3.6 copy.118
  75.7 3.6 copy.117
  79.3 5.0 subtract_convert_fusion.2
  86.7 5.4 all-gather.1
  93.4 3.6 convert_reduce_fusion.1
  97.0 2.3 copy.119
  99.3 3.2 slice.123
  102.5 2.6 copy.121
  105.1 3.7 maximum_bitcast_fusion
  110.3 3.2 fusion.84
  113.5 3.7 fusion.83
  117.2 95.4 %while.32 = (s32[]{:T(128)}, bf16[12,1,1024,64]{2,3,1,0:T(8,128)(2,1)}, f32[12,1,8,128]{3,2,1,0:T(8,128)S(1)}, bf16[12,1,1024,64]{2,3,1,0:T(8,128)(2,1)}, bf16[1...) while((s32[]{:T(128)}, ...), condition=%wide.region_7.8_spmd.clone, body=%wide.region_2.7_spmd.sunk.clone | while | flops 311426048 | bytes 18022532 | solution.py:314
  130.4 1.9 fusion.228
  212.6 5.2 fusion.127
  219.5 2.0 fusion.75
  221.5 13.2 %multiply_convert_fusion.2 = (bf16[1024,3072]{1,0:T(8,128)(2,1)}, f32[1024,3072]{1,0:T(8,128)}) fusion(f32[3072]{0:T(1024)S(1)} %bitcast.467, bf16[1024,768]{1,0:T(8,128)(2,1)} %fusion.75, bf16[768,3072]{1,0:T(8,128)(2,1)} %all-gather.14.cloned.1.call-done), kind=kOutput, calls=%fused_computation.96 | convolution fusion | flops 4863295488 | bytes 25178112 | tf_op jit(solution)/shard_map/dot_general | solution.py:52
  234.7 16.7 %convert_reduce_fusion = (f32[3072]{0:T(1024)S(1)}, bf16[1024,3072]{1,0:T(8,128)(2,1)}) fusion(f32[1024,3072]{1,0:T(8,128)} %get-tuple-element.336, f32[3072]{0:T(1024)S(1)} %bitcast.468, bf16[1024,768]{1,0:T(8,128)(2,1)S(1)} %copy-done.22, bf16[3072,768]{1,0:T(8,128)(2,1)} %all-gather.16.cloned.1.call-done), kind=kOutput, calls=%fused_computation.95 | convolution fusion | flops 4904186880 | bytes 25190400 | tf_op jit(solution)/shard_map/dot_general | solution.py:56
  251.4 9.5 multiply_reduce_fusion.3
  261.1 8.2 fusion.68
  269.3 2.6 convolution_convert_fusion
  271.9 188.7 %while.33 = (s32[]{:T(128)}, f32[12,1,1024,64]{2,3,1,0:T(8,128)}, f32[12,1,1024,64]{2,3,1,0:T(8,128)}, f32[12,1,1024,64]{2,3,1,0:T(8,128)}, f32[12,1,1024,64]{2,...) while((s32[]{:T(128)}, f32[12,1,1024,64]{2,3,1,0:T(8,128)}, ...), condition=%wide.region_15.16_spmd.clone, body=%wide.region_12.15_spmd.sunk.clone | while | flops 768998400 | bytes 45928640 | solution.py:364
  279.3 2.1 multiply_reduce_fusion.20
  295.0 2.1 multiply_reduce_fusion.20
  310.7 2.1 multiply_reduce_fusion.20
  326.4 2.1 multiply_reduce_fusion.20
  342.1 2.1 multiply_reduce_fusion.20
  357.8 2.1 multiply_reduce_fusion.20
  373.5 2.1 multiply_reduce_fusion.20
  389.2 2.1 multiply_reduce_fusion.20
  404.9 2.1 multiply_reduce_fusion.20
  420.7 2.1 multiply_reduce_fusion.20
  436.4 2.1 multiply_reduce_fusion.20
  452.1 2.1 multiply_reduce_fusion.20
  460.6 3.4 slice_select_fusion.1
  464.3 2.4 slice_select_fusion
  467.0 2.8 fusion.134
  469.8 2.1 bitcast_reduce_fusion
  472.2 2.9 select_add_fusion.1
  480.5 4.2 select_add_fusion
  488.1 5.1 multiply_reduce_fusion.4
  493.5 2.8 copy-done.8
  496.3 4.3 multiply_reduce_fusion.6
  501.1 2.5 fusion.87
  504.0 9.6 fusion.81
  513.7 10.3 fusion.136
  524.0 9.9 fusion.135
  537.8 3.8 reduce-scatter.14.cloned.1.call-done
  541.6 66.2 %reduce-scatter.6.cloned.1.call-done = f32[192,2304]{1,0:T(8,128)} async-done(((f32[768,2304]{1,0:T(8,128)}), f32[192,2304]{1,0:T(8,128)}) %reduce-scatter.6.cloned.1.call-update) | async-done | bytes 1769488 | tf_op jit(solution)/shard_map/reduce_scatter | solution.py:443
  607.8 81.2 %reduce-scatter.12.cloned.1.call-done = f32[768,768]{1,0:T(8,128)} async-done(((f32[3072,768]{1,0:T(8,128)}), f32[768,768]{1,0:T(8,128)}) %reduce-scatter.12.cloned.1.call-update) | async-done | bytes 2359312 | tf_op jit(solution)/shard_map/reduce_scatter | solution.py:446
  689.0 81.1 %reduce-scatter.10.cloned.1.call-done = f32[192,3072]{1,0:T(8,128)} async-done(((f32[768,3072]{1,0:T(8,128)}), f32[192,3072]{1,0:T(8,128)}) %reduce-scatter.10.cloned.1.call-update) | async-done | bytes 2359312 | tf_op jit(solution)/shard_map/reduce_scatter | solution.py:445
  772.1 4.8 select_reduce_fusion
  776.9 11.8 %all-reduce.14 = (f32[768]{0:T(1024)S(1)}, f32[768]{0:T(1024)S(1)}, f32[3072]{0:T(1024)S(1)}, f32[768]{0:T(1024)S(1)}, f32[4608]{0:T(1024)S(1)}, /*index=5*/f32[768]{0:T(1024)S(1)}) all-reduce(f32[768]{0:T(1024)S(1)} %get-tuple-element.202, f32[768]{0:T(1024)S(1)} %get-tuple-element.200, ...), channel_id=7, replica_groups=mesh['rep'=8,'shard'=4] {'shard'}, use_global_device_ids=true, to_apply=%region_36.37.clone | all-reduce | flops 10752 | bytes 86016
  789.2 34.4 %all-reduce.12 = (f32[192]{0:T(256)}, f32[192]{0:T(256)}, f32[768]{0:T(1024)}, f32[192]{0:T(256)}, f32[1152]{0:T(1024)}, /*index=5*/f32[192]{0:T(256)}) all-reduce(f32[192]{0:T(256)S(1)} %dynamic-slice.5, f32[192]{0:T(256)S(1)} %dynamic-slice.7, f32[768]{0:T(1024)S(1)} %dynamic-slice.9, ...), channel_id=1, replica_groups=mesh['rep'=8,'shard'=4] {'rep'}, use_global_device_ids=true, to_apply=%region_37.38 | all-reduce | flops 2688 | bytes 21504 | tf_op jit(solution)/shard_map/psum | solution.py:455
  823.6 3.8 broadcast_select_fusion
  827.4 78.2 %all-reduce.19.cloned.1.call-done = f32[1000,128]{1,0:T(8,128)} async-done(((f32[1000,128]{1,0:T(8,128)}), f32[1000,128]{1,0:T(8,128)}) %all-reduce.19.cloned.1.call-update) | async-done | bytes 512016 | tf_op jit(solution)/shard_map/psum | solution.py:428
  905.6 254.9 %all-reduce.21.cloned.1.call-done = (f32[192,2304]{1,0:T(8,128)}, f32[192,768]{1,0:T(8,128)}, f32[192,3072]{1,0:T(8,128)}, f32[768,768]{1,0:T(8,128)}, f32[32,4608]{1,0:T(8,128)}) async-done(((f32[192,2304]{1,0:T(8,128)}, f32[192,768]{1,0:T(8,128)}, f32[192,3072]{1,0:T(8,128)}, f32[768,768]{1,0:T(8,128)}, f32[32,4608]{1,0:T(8,128)}), (f32[192,2304]{1,0:T(8,128)}, f32[192,768]{1,0:T(8,128)}, ...) | async-done | bytes 7667728 | tf_op jit(solution)/shard_map/psum | solution.py:455
  1160.5 2.0 copy.319
  1162.5 2.8 copy.320
  (783 shorter events, 299.0 us)
Async XLA Ops:
  7.2 25.6 %copy-start = (f32[1000,128]{1,0:T(8,128)S(1)}, f32[1000,128]{1,0:T(8,128)}, u32[]{:S(2)}) copy-start(f32[1000,128]{1,0:T(8,128)} %param.23) | copy-start | bytes 1536004
  7.2 21.7 %copy-start.2 = (bf16[1024,768]{1,0:T(8,128)(2,1)S(1)}, bf16[1024,768]{1,0:T(8,128)(2,1)}, u32[]{:S(2)}) copy-start(bf16[1024,768]{1,0:T(8,128)(2,1)} %param.20) | copy-start | bytes 4718596
  7.2 25.9 %all-gather.8.cloned.1.call-start = ((), (), s32[]{:S(2)}) async-start(), calls=%async_computation.5 | async-start | bytes 1474560 | tf_op jit(solution)/shard_map/all_gather | solution.py:214
  7.9 52.0 %all-gather.10.cloned.1.call-start = ((), (), s32[]{:S(2)}) async-start(), calls=%async_computation.6 | async-start | bytes 4423680 | tf_op jit(solution)/shard_map/all_gather | solution.py:210
  8.7 203.9 %all-gather.12.cloned.1.call-start = ((), (), s32[]{:S(2)}) async-start(), calls=%async_computation.7 | async-start | bytes 1474560 | tf_op jit(solution)/shard_map/all_gather | solution.py:211
  9.4 212.1 %all-gather.14.cloned.1.call-start = ((), (), s32[]{:S(2)}) async-start(), calls=%async_computation.8 | async-start | bytes 5898240 | tf_op jit(solution)/shard_map/all_gather | solution.py:212
  10.0 224.7 %all-gather.16.cloned.1.call-start = ((), (), s32[]{:S(2)}) async-start(), calls=%async_computation.9 | async-start | bytes 5898240 | tf_op jit(solution)/shard_map/all_gather | solution.py:213
  21.5 13.5 %copy-start.40 = (f32[768]{0:T(1024)}, f32[768]{0:T(1024)S(1)}, u32[]{:S(2)}) copy-start(f32[768]{0:T(1024)S(1)} %convert_element_type.148) | copy-start | bytes 9220
  27.5 7.1 copy-start.51
  28.2 6.4 copy-start.48
  30.1 7.1 copy-start.38
  31.5 5.7 copy-start.42
  32.7 46.5 %copy-start.28 = (f32[1024,32]{0,1:T(8,128)}, f32[1024,32]{0,1:T(8,128)S(1)}, u32[]{:S(2)}) copy-start(f32[1024,32]{0,1:T(8,128)S(1)} %get-tuple-element.318) | copy-start | bytes 393220
  34.9 31.3 %copy-start.34 = (f32[8,768]{1,0:T(8,128)}, f32[8,768]{1,0:T(8,128)S(1)}, u32[]{:S(2)}) copy-start(f32[8,768]{1,0:T(8,128)S(1)} %get-tuple-element.314) | copy-start | bytes 73732
  66.3 5.9 copy-start.13
  67.5 41.3 %collective-permute-start.1 = (bf16[1,512,768]{2,1,0:T(8,128)(2,1)}, bf16[1,512,768]{2,1,0:T(8,128)(2,1)}, u32[]{:S(2)}, u32[]{:S(2)}) collective-permute-start(bf16[1,512,768]{2,1,0:T(8,128)(2,1)} %slice.81), channel_id=1, source_target_pairs={{0,1},{1,0},{2,3},{3,2},{4,5},{5,4},{6,7},{7,6},{8,9},{9,8},{10,11... | collective-permute-start | bytes 2359304 | tf_op jit(solution)/shard_map/ppermute | solution.py:24
  84.2 2.4 copy-start.50
  86.3 27.2 %collective-permute-start = (bf16[1,512,768]{1,2,0:T(8,128)(2,1)}, bf16[1,512,768]{1,2,0:T(8,128)(2,1)}, u32[]{:S(2)}, u32[]{:S(2)}) collective-permute-start(bf16[1,512,768]{1,2,0:T(8,128)(2,1)} %slice.79), channel_id=1, source_target_pairs={{0,1},{1,0},{2,3},{3,2},{4,5},{5,4},{6,7},{7,6},{8,9},{9,8},{10,11... | collective-permute-start | bytes 2359304 | tf_op jit(solution)/shard_map/ppermute | solution.py:24
  86.5 451.2 %reduce-scatter.8.cloned.1.call-start = ((), (), s32[]{:S(2)}) async-start(), calls=%async_computation.12 | async-start | bytes 2949120 | tf_op jit(solution)/shard_map/reduce_scatter | solution.py:444
  221.5 13.2 %copy-start.22 = (bf16[1024,768]{1,0:T(8,128)(2,1)S(1)}, bf16[1024,768]{1,0:T(8,128)(2,1)}, u32[]{:S(2)}) copy-start(bf16[1024,768]{1,0:T(8,128)(2,1)} %get-tuple-element.276) | copy-start | bytes 4718596
  234.7 16.7 %copy-start.5 = (f32[1024,768]{1,0:T(8,128)S(1)}, f32[1024,768]{1,0:T(8,128)}, u32[]{:S(2)}) copy-start(f32[1024,768]{1,0:T(8,128)} %copy-done.4) | copy-start | bytes 9437188
  251.4 9.6 slice-start
  251.4 9.6 slice-start.2
  251.4 9.6 copy-start.9
  251.4 9.6 slice-start.1
  251.4 9.6 slice-start.3
  261.0 8.3 copy-start.7
  261.1 8.3 copy-start.30
  269.3 2.6 copy-start.26
  460.6 3.7 copy-start.45
  464.0 3.0 copy-start.15
  464.0 3.0 copy-start.27
  464.0 8.1 collective-permute-start.2
  466.7 13.8 %collective-permute-start.3 = (f32[1,512,768]{1,2,0:T(8,128)S(1)}, f32[1,512,768]{1,2,0:T(8,128)}, u32[]{:S(2)}, u32[]{:S(2)}) collective-permute-start(f32[1,512,768]{1,2,0:T(8,128)S(1)} %slice_select_fusion), channel_id=1, source_target_pairs={{0,1},{1,0},{2,3},{3,2},{4,5},{5,4},{6,7},{7,6},{8,9},{9,8},{10,11... | collective-permute-start | bytes 4718600 | tf_op jit(solution)/shard_map/ppermute | solution.py:24
  471.9 69.7 %reduce-scatter.14.cloned.1.call-start = ((), (), s32[]{:S(2)}) async-start(), calls=%async_computation.15 | async-start | bytes 2949120 | tf_op jit(solution)/shard_map/reduce_scatter | solution.py:447
  475.1 1.9 copy-start.18
  477.0 2.0 copy-start.19
  477.0 2.0 copy-start.29
  477.0 2.1 copy-start.33
  480.3 5.3 copy-start.23
  480.5 5.2 copy-start.24
  480.5 4.6 copy-start.17
  485.1 3.1 copy-start.53
  485.6 7.7 copy-start.25
  488.1 5.4 copy-start.10
  488.1 5.4 copy-start.11
  488.1 5.4 copy-start.12
  493.3 7.4 copy-start.6
  493.3 3.1 copy-start.8
  493.3 3.0 copy-start.46
  493.3 3.0 copy-start.47
  496.3 4.4 copy-start.52
  496.3 4.8 copy-start.37
  503.7 104.1 %reduce-scatter.6.cloned.1.call-start = ((), (), s32[]{:S(2)}) async-start(), calls=%async_computation.11 | async-start | bytes 8847360 | tf_op jit(solution)/shard_map/reduce_scatter | solution.py:443
  513.6 175.4 %reduce-scatter.12.cloned.1.call-start = ((), (), s32[]{:S(2)}) async-start(), calls=%async_computation.14 | async-start | bytes 11796480 | tf_op jit(solution)/shard_map/reduce_scatter | solution.py:446
  524.0 246.1 %reduce-scatter.10.cloned.1.call-start = ((), (), s32[]{:S(2)}) async-start(), calls=%async_computation.13 | async-start | bytes 11796480 | tf_op jit(solution)/shard_map/reduce_scatter | solution.py:445
  533.9 2.3 copy-start.49
  533.9 371.7 %all-reduce.19.cloned.1.call-start = ((), (), s32[]{:S(2)}) async-start(), calls=%async_computation.10 | async-start | bytes 1024000 | tf_op jit(solution)/shard_map/psum | solution.py:428
  537.7 622.8 %all-reduce.21.cloned.1.call-start = ((), (), s32[]{:S(2)}) async-start(), calls=%async_computation.16 | async-start | bytes 15335424 | tf_op jit(solution)/shard_map/psum | solution.py:455
  772.1 4.8 copy-start.44
  1160.5 4.8 copy-start.32
  1160.5 5.6 copy-start.21
  1165.3 2.2 copy-start.20
  1166.1 3.7 copy-start.1
  (10 other events, 14.0 us)
Sparse Core Ops, SparseCore 0:
  9.6 17.9 all-gather.7
  29.2 30.6 all-gather.9
  61.5 17.5 all-gather.11
  80.5 37.4 all-gather.13
  119.4 37.4 all-gather.15
  472.0 33.1 reduce-scatter.7
  508.4 33.0 reduce-scatter.13
  544.1 63.6 reduce-scatter.5
  610.6 78.3 reduce-scatter.11
  691.6 78.4 reduce-scatter.9
  776.8 128.7 all-reduce.18
  910.5 249.9 all-reduce.20
where the time goes:
time: 1190 us; the launch traced here: 1180 us
  waiting for transfers between devices  591 us (50%)
  matrix products  270 us (23%)
  local copies, waits for them, and re-layouts  143 us (12%)
  other arithmetic  87.3 us (7%)
  blocking collectives  62.8 us (5%)
  between operations  18.1 us (2%)
    psum x1, waiting for transfers between devices, on_device(): lax.psum((shares[0], shares[1], shares[2], shares[3], shares[4], shares[5...  255 us
    reduce_scatter x1, waiting for transfers between devices, on_device(): lax.psum_scatter(grads[3], 'shard', scatter_dimension=0, tiled=True)  81.2 us
    reduce_scatter x1, waiting for transfers between devices, on_device(): lax.psum_scatter(grads[2], 'shard', scatter_dimension=0, tiled=True)  81.1 us
    psum x1, waiting for transfers between devices, on_device(): grad_time = lax.psum(table_term, ('rep', 'shard'))  78.2 us
    reduce_scatter x1, waiting for transfers between devices, on_device(): lax.psum_scatter(grads[0], 'shard', scatter_dimension=0, tiled=True)  66.2 us
    while x132, local copies, waits for them, and re-layouts  48.4 us
    dot_general x5, matrix products, product(): return jnp.dot(left_mat, right_mat, preferred_element_type=jnp.float32)  34.5 us
    psum x1, blocking collectives, on_device(): lax.psum((shares[0], shares[1], shares[2], shares[3], shares[4], shares[5...  34.4 us
  transfers between devices with their start and end apart: 16, of which 7 were waited for; matrix products, arithmetic and copies ran while one was open for 21% of the time, Pallas kernels for 0%

commit v1 on v0

--- a/solution.py
+++ b/solution.py
@@ -22,6 +22,62 @@
     mask = 2**apart
     pairs = [(source, source ^ mask) for source in range(lax.axis_size(axis))]
     return lax.ppermute(value, axis, pairs)
+
+
+def bit_masks(size):
+    count = size.bit_length() - 1
+    return [1 << k if k < 2 else 3 << (k - 1) for k in range(count)]
+
+
+def swap(value, axis, mask):
+    pairs = [(source, source ^ mask) for source in range(lax.axis_size(axis))]
+    return lax.ppermute(value, axis, pairs)
+
+
+def gather_rows(piece):
+    size = lax.axis_size("shard")
+    mine = lax.axis_index("shard")
+    pieces = {0: piece}
+    mask = size // 2
+    while mask:
+        for offset in list(pieces):
+            pieces[offset | mask] = swap(pieces[offset], "shard", mask)
+        mask //= 2
+    rows = piece.shape[0]
+    whole = jnp.zeros((rows * size,) + piece.shape[1:], piece.dtype)
+    for offset, part in pieces.items():
+        whole = lax.dynamic_update_slice_in_dim(whole, part, (mine ^ offset) * rows, 0)
+    return whole
+
+
+def reduce_weight(grad):
+    size = lax.axis_size("shard")
+    mine = lax.axis_index("shard")
+    rows, width = grad.shape[0] // size, grad.shape[1]
+    value = grad.astype(jnp.bfloat16)
+    mask = 1
+    while mask < size:
+        bit = (mine // mask) % 2
+        halves = value.reshape(-1, 2, rows, width)
+        keep = lax.dynamic_index_in_dim(halves, bit, 1, False)
+        send = lax.dynamic_index_in_dim(halves, 1 - bit, 1, False)
+        got = swap(send, "shard", mask)
+        value = (keep.astype(jnp.float32) + got.astype(jnp.float32)).astype(jnp.bfloat16)
+        mask *= 2
+    value = value.reshape(rows, width)
+    for step in bit_masks(lax.axis_size("rep")):
+        got = swap(value, "rep", step)
+        total = value.astype(jnp.float32) + got.astype(jnp.float32)
+        value = total.astype(jnp.bfloat16)
+    return total
+
+
+def reduce_small(values):
+    for mask in bit_masks(lax.axis_size("shard")):
+        values = values + swap(values, "shard", mask)
+    for mask in bit_masks(lax.axis_size("rep")):
+        values = values + swap(values, "rep", mask)
+    return values
 
 
 def layer_norm(values):
@@ -193,45 +249,22 @@
     mask_embed,
     cotangent,
 ):
-    sharded = (
-        w_qkv,
-        w_proj,
-        w_up,
-        w_down,
-        w_ada,
-        gain_attn,
-        gain_mlp,
-        bias_up,
-        bias_down,
-        bias_ada,
-        mask_embed,
-    )
-    gathered = (
-        lax.all_gather(sharded[0], "shard", axis=0, tiled=True),
-        lax.all_gather(sharded[1], "shard", axis=0, tiled=True),
-        lax.all_gather(sharded[2], "shard", axis=0, tiled=True),
-        lax.all_gather(sharded[3], "shard", axis=0, tiled=True),
-        lax.all_gather(sharded[4], "shard", axis=0, tiled=True),
-        lax.all_gather(sharded[5], "shard", axis=0, tiled=True),
-        lax.all_gather(sharded[6], "shard", axis=0, tiled=True),
-        lax.all_gather(sharded[7], "shard", axis=0, tiled=True),
-        lax.all_gather(sharded[8], "shard", axis=0, tiled=True),
-        lax.all_gather(sharded[9], "shard", axis=0, tiled=True),
-        lax.all_gather(sharded[10], "shard", axis=0, tiled=True),
-    )
-    (
-        qkv_mat,
-        proj_mat,
-        up_mat,
-        down_mat,
-        ada_mat,
-        attn_gain,
-        mlp_gain,
-        up_bias,
-        down_bias,
-        ada_bias,
-        embed_vec,
-    ) = gathered
+    vectors = (gain_attn, gain_mlp, bias_up, bias_down, bias_ada, mask_embed)
+    lengths = [v.shape[0] for v in vectors]
+    row = jnp.pad(jnp.concatenate(vectors), (0, w_ada.shape[1] - sum(lengths)))
+    n_shard = lax.axis_size("shard")
+    packed = gather_rows(jnp.concatenate([w_ada, row[None]], 0)[None])
+    ada_mat = packed[:, :-1].reshape(-1, w_ada.shape[1])
+    full_vectors = []
+    start_at = 0
+    for length in lengths:
+        full_vectors.append(packed[:, -1, start_at : start_at + length].reshape(-1))
+        start_at += length
+    attn_gain, mlp_gain, up_bias, down_bias, ada_bias, embed_vec = full_vectors
+    qkv_mat = gather_rows(w_qkv)
+    proj_mat = gather_rows(w_proj)
+    up_mat = gather_rows(w_up)
+    down_mat = gather_rows(w_down)
     shard_index = lax.axis_index("shard")
     rep_index = lax.axis_index("rep")
     half_index = shard_index % 2
@@ -327,20 +360,7 @@
     act_low = act_value.astype(jnp.bfloat16)
     mlp_out = (product(act_low, down_mat) + down_bias.astype(jnp.float32)).reshape(shape_four)
     block_out = (middle + gate_mlp * mlp_out).astype(jnp.bfloat16).reshape(tok_count, D)
-    back_weights = (
-        lax.all_gather(sharded[0], "shard", axis=0, tiled=True),
-        lax.all_gather(sharded[1], "shard", axis=0, tiled=True),
-        lax.all_gather(sharded[2], "shard", axis=0, tiled=True),
-        lax.all_gather(sharded[3], "shard", axis=0, tiled=True),
-        lax.all_gather(sharded[4], "shard", axis=0, tiled=True),
-        lax.all_gather(sharded[5], "shard", axis=0, tiled=True),
-        lax.all_gather(sharded[6], "shard", axis=0, tiled=True),
-        lax.all_gather(sharded[7], "shard", axis=0, tiled=True),
-        lax.all_gather(sharded[8], "shard", axis=0, tiled=True),
-        lax.all_gather(sharded[9], "shard", axis=0, tiled=True),
-        lax.all_gather(sharded[10], "shard", axis=0, tiled=True),
-    )
-    qkv_back, proj_back, up_back, down_back, ada_back = back_weights[:5]
+    qkv_back, proj_back, up_back, down_back, ada_back = qkv_mat, proj_mat, up_mat, down_mat, ada_mat
     grad_top = cotangent.astype(jnp.float32).reshape(shape_four)
     grad_gate_mlp = jnp.sum(grad_top * mlp_out, 2)
     grad_branch = (gate_mlp * grad_top).astype(jnp.bfloat16).reshape(tok_count, D)
@@ -422,16 +442,7 @@
         precision=lax.Precision.HIGHEST,
     )
     grad_cond = silu_back(grad_silu)[0]
-    table_term = lax.dot_general(
-        one_hot, grad_cond, (((0,), (0,)), ((), ())), precision=lax.Precision.HIGHEST
-    )
-    grad_time = lax.psum(table_term, ("rep", "shard"))
-    grads = (
-        grad_qkv,
-        grad_proj,
-        grad_up,
-        grad_down,
-        grad_ada,
+    small = (
         grad_gain_attn,
         grad_gain_mlp,
         grad_bias_up,
@@ -439,36 +450,38 @@
         grad_bias_ada,
         grad_mask_embed,
     )
-    shares = (
-        lax.psum_scatter(grads[0], "shard", scatter_dimension=0, tiled=True),
-        lax.psum_scatter(grads[1], "shard", scatter_dimension=0, tiled=True),
-        lax.psum_scatter(grads[2], "shard", scatter_dimension=0, tiled=True),
-        lax.psum_scatter(grads[3], "shard", scatter_dimension=0, tiled=True),
-        lax.psum_scatter(grads[4], "shard", scatter_dimension=0, tiled=True),
-        lax.psum_scatter(grads[5], "shard", scatter_dimension=0, tiled=True),
-        lax.psum_scatter(grads[6], "shard", scatter_dimension=0, tiled=True),
-        lax.psum_scatter(grads[7], "shard", scatter_dimension=0, tiled=True),
-        lax.psum_scatter(grads[8], "shard", scatter_dimension=0, tiled=True),
-        lax.psum_scatter(grads[9], "shard", scatter_dimension=0, tiled=True),
-        lax.psum_scatter(grads[10], "shard", scatter_dimension=0, tiled=True),
-    )
-    summed = lax.psum(
-        (
-            shares[0],
-            shares[1],
-            shares[2],
-            shares[3],
-            shares[4],
-            shares[5],
-            shares[6],
-            shares[7],
-            shares[8],
-            shares[9],
-            shares[10],
-        ),
-        "rep",
-    )
-    return (block_out, grad_hidden, grad_time) + tuple(summed)
+    small_rows = jnp.concatenate(small).reshape(-1, 128)
+    n_rows = small_rows.shape[0]
+    all_rows = jnp.zeros((n_rows + time_ids.size, 128), jnp.float32)
+    all_rows = lax.dynamic_update_slice_in_dim(all_rows, small_rows, 0, 0)
+    all_rows = lax.dynamic_update_slice_in_dim(
+        all_rows, grad_cond, n_rows + pair_index * grad_cond.shape[0], 0
+    )
+    all_rows = reduce_small(all_rows)
+    hot_all = (time_ids.reshape(-1)[:, None] == jnp.arange(STEPS, dtype=jnp.int32)[None, :]).astype(
+        jnp.float32
+    )
+    grad_time = lax.dot_general(
+        hot_all, all_rows[n_rows:], (((0,), (0,)), ((), ())), precision=lax.Precision.HIGHEST
+    )
+    flat = all_rows[:n_rows].reshape(-1)
+    small_out = []
+    start_at = 0
+    for value in small:
+        length = value.shape[0]
+        part = flat[start_at : start_at + length].reshape(n_shard, -1)
+        small_out.append(lax.dynamic_index_in_dim(part, shard_index, 0, False))
+        start_at += length
+    return (
+        block_out,
+        grad_hidden,
+        grad_time,
+        reduce_weight(grad_qkv),
+        reduce_weight(grad_proj),
+        reduce_weight(grad_up),
+        reduce_weight(grad_down),
+        reduce_weight(grad_ada),
+    ) + tuple(small_out)
 
 
 def solution(mesh):

time: 1190 us -> 912 us (0.77)
  waiting for transfers between devices: 591 us -> 292 us
  blocking collectives: 62.8 us -> 0 us
  local copies, waits for them, and re-layouts: 143 us -> 187 us
  starting transfers between devices: 2 us -> 41.4 us
  between operations: 18.1 us -> 2.16 us
  other arithmetic: 87.3 us -> 103 us
    psum x2 -> x0, waiting for transfers between devices: 333 us -> none  [the longest x1 255 us: on_device(): lax.psum((shares[0], shares[1], shares[2], shares[3], shares[4], shares[5...]
    ppermute x0 -> x45, waiting for transfers between devices: none -> 292 us  [swap(): return lax.ppermute(value, axis, pairs)]
    reduce_scatter x5 -> x0, waiting for transfers between devices: 232 us -> none  [the longest x1 81.2 us: on_device(): lax.psum_scatter(grads[3], 'shard', scatter_dimension=0, tiled=True)]
    ppermute x0 -> x45, starting transfers between devices: none -> 40.6 us  [swap(): return lax.ppermute(value, axis, pairs)]
    psum x1 -> x0, blocking collectives: 34.4 us -> none  [on_device(): lax.psum((shares[0], shares[1], shares[2], shares[3], shares[4], shares[5...]
    dynamic_update_slice x0 -> x21, local copies, waits for them, and re-layouts: none -> 27.6 us  [the longest x19 25.5 us: gather_rows(): lax.dynamic_update_slice_in_dim(whole, part, (mine ^ offset) * rows, 0)]
    all_gather x5 -> x0, waiting for transfers between devices: 22.8 us -> none  [the longest x1 22.7 us: on_device(): lax.all_gather(sharded[0], 'shard', axis=0, tiled=True)]
    unnamed x144 -> x154, local copies, waits for them, and re-layouts: 27.8 us -> 7.74 us
  transfers between devices with their start and end apart: 16 -> 49, of which waited for: 7 -> 21; matrix products, arithmetic and copies ran while one was open for 21% -> 19% of each run, Pallas kernels for 0% -> 0%
where the time goes in v1:
time: 912 us; the launch traced here: 903 us
  waiting for transfers between devices  292 us (32%)
  matrix products  275 us (30%)
  local copies, waits for them, and re-layouts  187 us (21%)
  other arithmetic  103 us (11%)
  starting transfers between devices  41.4 us (5%)
    ppermute x45, waiting for transfers between devices, swap(): return lax.ppermute(value, axis, pairs)  292 us
    while x132, local copies, waits for them, and re-layouts  48.3 us
    ppermute x45, starting transfers between devices, swap(): return lax.ppermute(value, axis, pairs)  40.6 us
    dot_general x5, matrix products, product(): return jnp.dot(left_mat, right_mat, preferred_element_type=jnp.float32)  39.9 us
    dot_general x4, matrix products, times_trans(): lax.dot_general(left_mat, right_mat, (((1,), (1,)), ((), ())), preferred_...  35.9 us
    dynamic_update_slice x48, local copies, waits for them, and re-layouts, on_device(): attn_out, log_sum = lax.map(head_forward, operands)  34.4 us
    dot_general x4, matrix products, contract(): lax.dot_general(left_mat, right_mat, (((0,), (0,)), ((), ())), preferred_...  31.5 us
    dynamic_update_slice x19, local copies, waits for them, and re-layouts, gather_rows(): lax.dynamic_update_slice_in_dim(whole, part, (mine ^ offset) * rows, 0)  25.5 us
  transfers between devices with their start and end apart: 49, of which 21 were waited for; matrix products, arithmetic and copies ran while one was open for 19% of the time, Pallas kernels for 0%

profile of v1, /device:TPU:10, one launch (start us, length us, event | category | flops | bytes accessed | tf_op | source)
XLA Modules:
  0.0 903.4 jit_solution(316504645795567558)
XLA Ops:
  1.4 4.1 concatenate.119
  17.9 2.8 broadcast_in_dim.153
  21.8 2.5 broadcast_in_dim.154
  44.4 2.1 convert_reduce_fusion.1
  50.1 2.2 constant_dynamic-update-slice_fusion.19
  52.2 2.1 constant_dynamic-update-slice_fusion.18
  54.4 20.0 %collective-permute-done.11 = bf16[192,3072]{1,0:T(8,128)(2,1)} collective-permute-done((bf16[192,3072]{1,0:T(8,128)(2,1)}, bf16[192,3072]{1,0:T(8,128)(2,1)}, u32[]{:S(2)}, u32[]{:S(2)}) %collective-permute-start.11) | collective-permute-done | bytes 1179680 | tf_op jit(solution)/shard_map/ppermute | solution.py:34
  74.4 24.4 %collective-permute-done.14 = bf16[768,768]{1,0:T(8,128)(2,1)} collective-permute-done((bf16[768,768]{1,0:T(8,128)(2,1)}, bf16[768,768]{1,0:T(8,128)(2,1)}, u32[]{:S(2)}, u32[]{:S(2)}) %collective-permute-start.14) | collective-permute-done | bytes 1179680 | tf_op jit(solution)/shard_map/ppermute | solution.py:34
  98.8 2.3 constant_dynamic-update-slice_fusion.7
  101.1 2.4 constant_dynamic-update-slice_fusion.6
  103.5 2.4 constant_dynamic-update-slice_fusion.11
  108.0 5.8 fusion.147
  113.8 3.3 fusion.144
  120.9 2.4 copy.81
  123.3 3.2 slice.224
  126.4 3.5 copy.80
  129.9 2.6 copy.83
  132.6 3.5 copy.79
  136.1 3.9 subtract_convert_fusion.2
  143.7 2.4 constant_dynamic-update-slice_fusion.5
  146.2 2.4 constant_dynamic-update-slice_fusion.9
  148.6 2.3 copy.82
  150.8 3.8 fusion.86
  154.6 3.7 fusion.85
  158.3 102.7 %while.32 = (s32[]{:T(128)}, bf16[12,1,1024,64]{2,3,1,0:T(8,128)(2,1)}, f32[12,1,8,128]{3,2,1,0:T(8,128)}, bf16[12,1,1024,64]{2,3,1,0:T(8,128)(2,1)}, bf16[12,1,...) while((s32[]{:T(128)}, ...), condition=%wide.region_7.8_spmd.clone, body=%wide.region_2.7_spmd.sunk.clone | while | flops 311426048 | bytes 18022532 | solution.py:347
  261.0 5.2 fusion.141
  268.7 10.9 %fusion.148 = f32[1024,3072]{1,0:T(8,128)} fusion(bf16[1024,768]{1,0:T(8,128)(2,1)S(1)} %fusion.78, bf16[768,3072]{1,0:T(8,128)(2,1)} %constant_dynamic-update-slice_fusion.9), kind=kOutput, calls=%fused_computation.352 | convolution fusion | flops 4831838208 | bytes 18874368 | tf_op jit(solution)/shard_map/dot_general | solution.py:108
  279.7 12.3 %convolution_convert_fusion.1 = bf16[3072,768]{1,0:T(8,128)(2,1)} fusion(bf16[1024,768]{1,0:T(8,128)(2,1)S(1)} %copy-done.26, f32[1024,3072]{1,0:T(8,128)} %fusion.148, f32[3072]{0:T(1024)S(1)} %bitcast.537), kind=kOutput, calls=%fused_computation.100 | convolution fusion | flops 4865654784 | bytes 18886656 | tf_op jit(solution)/shard_map/dot_general | solution.py:118
  292.0 16.0 %convert_reduce_fusion = (f32[3072]{0:T(1024)}, bf16[1024,3072]{1,0:T(8,128)(2,1)S(1)}) fusion(f32[1024,3072]{1,0:T(8,128)} %fusion.148, f32[3072]{0:T(1024)S(1)} %bitcast.538, bf16[1024,768]{1,0:T(8,128)(2,1)S(1)} %copy-done.26, bf16[3072,768]{1,0:T(8,128)(2,1)} %constant_dynamic-update-slice_fusion.5), kind=kOutput, calls=%fused_computation.95 | convolution fusion | flops 4904186880 | bytes 25190400 | tf_op jit(solution)/shard_map/dot_general | solution.py:112
  308.0 10.4 %multiply_reduce_fusion.7 = (f32[768]{0:T(1024)S(1)}, f32[1024]{0:T(1024)S(1)}, f32[1024]{0:T(1024)S(1)}, f32[1024,768]{1,0:T(8,128)S(1)}) fusion(f32[1024,768]{1,0:T(8,128)S(1)} %get-tuple-element.242, f32[8,768]{1,0:T(8,128)S(1)} %get-tuple-element.274, f32[1024]{0:T(1024)S(1)} %get-tuple-element.294, f32[1024]{0:T(1024)S(1)} %get-tuple-element.296, ...), kind=kOutput, calls=%fused_computation.141 | convolution fusion | flops 4838913024 | bytes 17348608 | tf_op jit(solution)/shard_map/dot_general | solution.py:112
  318.4 16.4 %fusion.71 = (bf16[1024,768]{1,0:T(8,128)(2,1)S(1)}, f32[1024,768]{1,0:T(8,128)}, bf16[1024,768]{1,0:T(8,128)(2,1)}, f32[1024,768]{1,0:T(8,128)}) fusion(f32[8,768]{1,0:T(8,128)S(1)} %get-tuple-element.277, f32[1024]{0:T(1024)S(1)} %get-tuple-element.292, f32[1024,768]{1,0:T(8,128)S(1)} %get-tuple-element.242, f32[1024]{0:T(1024)S(1)} %get-tuple-element.296, ...), kind=kOutput, calls=%fused_computation.119 | convolution fusion | flops 4875878400 | bytes 34711552 | tf_op jit(solution)/shard_map/dot_general | solution.py:108
  334.8 2.4 convolution_convert_fusion.5
  337.2 2.6 convolution_convert_fusion.4
  339.8 196.8 %while.33 = (s32[]{:T(128)}, f32[12,1,1024,64]{2,3,1,0:T(8,128)}, f32[12,1,1024,64]{2,3,1,0:T(8,128)}, f32[12,1,1024,64]{2,3,1,0:T(8,128)}, f32[12,1,1024,64]{2,...) while((s32[]{:T(128)}, f32[12,1,1024,64]{2,3,1,0:T(8,128)}, ...), condition=%wide.region_15.16_spmd.clone, body=%wide.region_12.15_spmd.sunk.clone | while | flops 768998400 | bytes 45928640 | solution.py:384
  396.9 2.1 multiply_reduce_fusion.20
  413.3 2.1 multiply_reduce_fusion.20
  429.7 2.1 multiply_reduce_fusion.20
  478.9 2.1 multiply_reduce_fusion.20
  538.3 7.9 convolution_convert_fusion.2
  549.1 3.0 slice_select_fusion
  552.2 5.6 collective-permute-done.30
  559.9 6.4 collective-permute-done.31
  568.7 5.2 collective-permute-done.32
  576.2 2.4 select_add_fusion
  586.1 7.0 multiply_reduce_fusion.8
  593.2 8.9 convolution_convert_fusion.3
  603.5 4.1 multiply_reduce_fusion.4
  617.2 4.0 collective-permute-done.20
  622.8 2.8 dynamic-slice_bitcast_fusion.10
  626.2 2.5 collective-permute-start.22
  633.7 6.0 collective-permute-done.23
  646.5 3.2 fusion.67
  651.1 2.7 fusion.68
  658.2 22.8 %collective-permute-done.40 = bf16[1,768,768]{2,1,0:T(8,128)(2,1)S(1)} collective-permute-done((bf16[1,768,768]{2,1,0:T(8,128)(2,1)S(1)}, bf16[1,768,768]{2,1,0:T(8,128)(2,1)S(1)}, u32[]{:S(2)}, u32[]{:S(2)}) %collective-permute-start.40) | collective-permute-done | bytes 1179680 | tf_op jit(solution)/shard_map/ppermute | solution.py:34
  683.0 23.4 %collective-permute-done.35 = bf16[1,192,3072]{2,1,0:T(8,128)(2,1)S(1)} collective-permute-done((bf16[1,192,3072]{2,1,0:T(8,128)(2,1)S(1)}, bf16[1,192,3072]{2,1,0:T(8,128)(2,1)S(1)}, u32[]{:S(2)}, u32[]{:S(2)}) %collective-permute-start.35) | collective-permute-done | bytes 1179680 | tf_op jit(solution)/shard_map/ppermute | solution.py:34
  709.9 12.2 %collective-permute-done.25 = bf16[1,192,2304]{2,1,0:T(8,128)(2,1)S(1)} collective-permute-done((bf16[1,192,2304]{2,1,0:T(8,128)(2,1)S(1)}, bf16[1,192,2304]{2,1,0:T(8,128)(2,1)S(1)}, u32[]{:S(2)}, u32[]{:S(2)}) %collective-permute-start.25) | collective-permute-done | bytes 884768 | tf_op jit(solution)/shard_map/ppermute | solution.py:34
  724.3 3.3 collective-permute-start.42
  727.7 7.3 collective-permute-done.36
  735.4 2.3 collective-permute-start.37
  737.8 9.7 %collective-permute-done.26 = bf16[192,2304]{1,0:T(8,128)(2,1)S(1)} collective-permute-done((bf16[192,2304]{1,0:T(8,128)(2,1)S(1)}, bf16[192,2304]{1,0:T(8,128)(2,1)S(1)}, u32[]{:S(2)}, u32[]{:S(2)}) %collective-permute-start.26) | collective-permute-done | bytes 884768 | tf_op jit(solution)/shard_map/ppermute | solution.py:34
  747.7 5.1 collective-permute-start.27
  756.0 29.2 %collective-permute-done.37 = bf16[192,3072]{1,0:T(8,128)(2,1)S(1)} collective-permute-done((bf16[192,3072]{1,0:T(8,128)(2,1)S(1)}, bf16[192,3072]{1,0:T(8,128)(2,1)S(1)}, u32[]{:S(2)}, u32[]{:S(2)}) %collective-permute-start.37) | collective-permute-done | bytes 1179680 | tf_op jit(solution)/shard_map/ppermute | solution.py:34
  785.7 19.5 %collective-permute-done.27 = bf16[192,2304]{1,0:T(8,128)(2,1)S(1)} collective-permute-done((bf16[192,2304]{1,0:T(8,128)(2,1)S(1)}, bf16[192,2304]{1,0:T(8,128)(2,1)S(1)}, u32[]{:S(2)}, u32[]{:S(2)}) %collective-permute-start.27) | collective-permute-done | bytes 884768 | tf_op jit(solution)/shard_map/ppermute | solution.py:34
  807.4 91.1 %collective-permute-done.28 = bf16[192,2304]{1,0:T(8,128)(2,1)S(1)} collective-permute-done((bf16[192,2304]{1,0:T(8,128)(2,1)S(1)}, bf16[192,2304]{1,0:T(8,128)(2,1)S(1)}, u32[]{:S(2)}, u32[]{:S(2)}) %collective-permute-start.28) | collective-permute-done | bytes 884768 | tf_op jit(solution)/shard_map/ppermute | solution.py:34
  (932 shorter events, 406.4 us)
Async XLA Ops:
  0.6 12.6 %copy-start = (f32[1000,128]{1,0:T(8,128)S(1)}, f32[1000,128]{1,0:T(8,128)}, u32[]{:S(2)}) copy-start(f32[1000,128]{1,0:T(8,128)} %param.23) | copy-start | bytes 1536004
  0.7 14.2 %copy-start.34 = (bf16[32,4608]{1,0:T(8,128)(2,1)S(1)}, bf16[32,4608]{1,0:T(8,128)(2,1)}, u32[]{:S(2)}) copy-start(bf16[32,4608]{1,0:T(8,128)(2,1)} %param.28) | copy-start | bytes 884740
  0.7 27.2 %collective-permute-start.9 = (bf16[192,768]{1,0:T(8,128)(2,1)}, bf16[192,768]{1,0:T(8,128)(2,1)}, u32[]{:S(2)}, u32[]{:S(2)}) collective-permute-start(bf16[192,768]{1,0:T(8,128)(2,1)} %param.25), channel_id=1, source_target_pairs={{0,1},{1,0},{2,3},{3,2},{4,5},{5,4},{6,7},{7,6},{8,9},{9,8},{10,11... | collective-permute-start | bytes 884744 | tf_op jit(solution)/shard_map/ppermute | solution.py:34
  0.8 25.5 %collective-permute-start.8 = (bf16[192,768]{1,0:T(8,128)(2,1)}, bf16[192,768]{1,0:T(8,128)(2,1)}, u32[]{:S(2)}, u32[]{:S(2)}) collective-permute-start(bf16[192,768]{1,0:T(8,128)(2,1)} %param.25), channel_id=1, source_target_pairs={{0,2},{1,3},{2,0},{3,1},{4,6},{5,7},{6,4},{7,5},{8,10},{9,11},{10,... | collective-permute-start | bytes 884744 | tf_op jit(solution)/shard_map/ppermute | solution.py:34
  7.2 23.1 %collective-permute-start = (bf16[1,33,4608]{2,1,0:T(8,128)(2,1)}, bf16[1,33,4608]{2,1,0:T(8,128)(2,1)}, u32[]{:S(2)}, u32[]{:S(2)}) collective-permute-start(bf16[1,33,4608]{2,1,0:T(8,128)(2,1)} %maximum_bitcast_fusion.2), channel_id=1, source_target_pairs={{0,2},{1,3},{2,0},{3,1},{4,6},{5,7},{6,4},{7,5},{8,10},{9,11},{10,... | collective-permute-start | bytes 912392 | tf_op jit(solution)/shard_map/ppermute | solution.py:34
  8.7 22.7 %collective-permute-start.1 = (bf16[1,33,4608]{2,1,0:T(8,128)(2,1)}, bf16[1,33,4608]{2,1,0:T(8,128)(2,1)}, u32[]{:S(2)}, u32[]{:S(2)}) collective-permute-start(bf16[1,33,4608]{2,1,0:T(8,128)(2,1)} %maximum_bitcast_fusion.2), channel_id=1, source_target_pairs={{0,1},{1,0},{2,3},{3,2},{4,5},{5,4},{6,7},{7,6},{8,9},{9,8},{10,11... | collective-permute-start | bytes 912392 | tf_op jit(solution)/shard_map/ppermute | solution.py:34
  8.7 43.5 %collective-permute-start.4 = (bf16[192,2304]{1,0:T(8,128)(2,1)}, bf16[192,2304]{1,0:T(8,128)(2,1)}, u32[]{:S(2)}, u32[]{:S(2)}) collective-permute-start(bf16[192,2304]{1,0:T(8,128)(2,1)} %param.24), channel_id=1, source_target_pairs={{0,1},{1,0},{2,3},{3,2},{4,5},{5,4},{6,7},{7,6},{8,9},{9,8},{10,11... | collective-permute-start | bytes 2654216 | tf_op jit(solution)/shard_map/ppermute | solution.py:34
  10.0 251.1 %copy-start.49 = (pred[1024]{0:T(1024)(128)(4,1)}, pred[1024]{0:T(1024)(128)(4,1)S(1)}, u32[]{:S(2)}) copy-start(pred[1024]{0:T(1024)(128)(4,1)S(1)} %broadcast_compare_fusion) | copy-start | bytes 3076
  13.6 24.1 %copy-start.42 = (f32[9,128]{1,0:T(8,128)}, f32[9,128]{1,0:T(8,128)S(1)}, u32[]{:S(2)}) copy-start(f32[9,128]{1,0:T(8,128)S(1)} %fusion.104) | copy-start | bytes 13828
  14.8 121.3 %copy-start.28 = (f32[1024,32]{0,1:T(8,128)}, f32[1024,32]{0,1:T(8,128)S(1)}, u32[]{:S(2)}) copy-start(f32[1024,32]{0,1:T(8,128)S(1)} %get-tuple-element.284) | copy-start | bytes 393220
  26.2 13.0 %copy-start.65 = (s32[8]{0:T(128)}, s32[8]{0:T(128)S(1)}, u32[]{:S(2)}) copy-start(s32[8]{0:T(128)S(1)} %compare_select_fusion) | copy-start | bytes 100
  26.2 23.3 %collective-permute-start.3 = (bf16[192,2304]{1,0:T(8,128)(2,1)}, bf16[192,2304]{1,0:T(8,128)(2,1)}, u32[]{:S(2)}, u32[]{:S(2)}) collective-permute-start(bf16[192,2304]{1,0:T(8,128)(2,1)} %param.24), channel_id=1, source_target_pairs={{0,2},{1,3},{2,0},{3,1},{4,6},{5,7},{6,4},{7,5},{8,10},{9,11},{10,... | collective-permute-start | bytes 2654216 | tf_op jit(solution)/shard_map/ppermute | solution.py:34
  27.8 46.6 %collective-permute-start.11 = (bf16[192,3072]{1,0:T(8,128)(2,1)}, bf16[192,3072]{1,0:T(8,128)(2,1)}, u32[]{:S(2)}, u32[]{:S(2)}) collective-permute-start(bf16[192,3072]{1,0:T(8,128)(2,1)} %param.26), channel_id=1, source_target_pairs={{0,2},{1,3},{2,0},{3,1},{4,6},{5,7},{6,4},{7,5},{8,10},{9,11},{10,... | collective-permute-start | bytes 3538952 | tf_op jit(solution)/shard_map/ppermute | solution.py:34
  30.4 2.7 collective-permute-start.10
  31.5 2.1 collective-permute-start.2
  33.1 68.0 %collective-permute-start.15 = (bf16[768,768]{1,0:T(8,128)(2,1)}, bf16[768,768]{1,0:T(8,128)(2,1)}, u32[]{:S(2)}, u32[]{:S(2)}) collective-permute-start(bf16[768,768]{1,0:T(8,128)(2,1)} %param.27), channel_id=1, source_target_pairs={{0,1},{1,0},{2,3},{3,2},{4,5},{5,4},{6,7},{7,6},{8,9},{9,8},{10,11... | collective-permute-start | bytes 3538952 | tf_op jit(solution)/shard_map/ppermute | solution.py:34
  33.6 65.2 %collective-permute-start.14 = (bf16[768,768]{1,0:T(8,128)(2,1)}, bf16[768,768]{1,0:T(8,128)(2,1)}, u32[]{:S(2)}, u32[]{:S(2)}) collective-permute-start(bf16[768,768]{1,0:T(8,128)(2,1)} %param.27), channel_id=1, source_target_pairs={{0,2},{1,3},{2,0},{3,1},{4,6},{5,7},{6,4},{7,5},{8,10},{9,11},{10,... | collective-permute-start | bytes 3538952 | tf_op jit(solution)/shard_map/ppermute | solution.py:34
  36.5 224.5 %copy-start.40 = (f32[768]{0:T(1024)}, f32[768]{0:T(1024)S(1)}, u32[]{:S(2)}) copy-start(f32[768]{0:T(1024)S(1)} %reshape.1431) | copy-start | bytes 9220
  48.1 59.8 %copy-start.24 = (bf16[1024,768]{1,0:T(8,128)(2,1)}, bf16[1024,768]{1,0:T(8,128)(2,1)S(1)}, u32[]{:S(2)}) copy-start(bf16[1024,768]{1,0:T(8,128)(2,1)S(1)} %fusion.73) | copy-start | bytes 4718596
  49.6 56.3 %collective-permute-start.12 = (bf16[192,3072]{1,0:T(8,128)(2,1)S(1)}, bf16[192,3072]{1,0:T(8,128)(2,1)S(1)}, u32[]{:S(2)}, u32[]{:S(2)}) collective-permute-start(bf16[192,3072]{1,0:T(8,128)(2,1)S(1)} %copy-done.32), channel_id=1, source_target_pairs={{0,1},{1,0},{2,3},{3,2},{4,5},{5,4},{6,7},{7,6},{8,9},{9,8},{10,11... | collective-permute-start | bytes 3538952 | tf_op jit(solution)/shard_map/ppermute | solution.py:34
  52.2 54.7 %collective-permute-start.5 = (bf16[192,2304]{1,0:T(8,128)(2,1)}, bf16[192,2304]{1,0:T(8,128)(2,1)S(1)}, u32[]{:S(2)}, u32[]{:S(2)}) collective-permute-start(bf16[192,2304]{1,0:T(8,128)(2,1)} %collective-permute-done.3), channel_id=1, source_target_pairs={{0,1},{1,0},{2,3},{3,2},{4,5},{5,4},{6,7},{7,6},{8,9},{9,8},{10,11... | collective-permute-start | bytes 2654216 | tf_op jit(solution)/shard_map/ppermute | solution.py:34
  74.4 71.8 %collective-permute-start.13 = (bf16[192,3072]{1,0:T(8,128)(2,1)}, bf16[192,3072]{1,0:T(8,128)(2,1)}, u32[]{:S(2)}, u32[]{:S(2)}) collective-permute-start(bf16[192,3072]{1,0:T(8,128)(2,1)} %collective-permute-done.11), channel_id=1, source_target_pairs={{0,1},{1,0},{2,3},{3,2},{4,5},{5,4},{6,7},{7,6},{8,9},{9,8},{10,11... | collective-permute-start | bytes 3538952 | tf_op jit(solution)/shard_map/ppermute | solution.py:34
  98.8 45.0 %collective-permute-start.16 = (bf16[768,768]{1,0:T(8,128)(2,1)}, bf16[768,768]{1,0:T(8,128)(2,1)}, u32[]{:S(2)}, u32[]{:S(2)}) collective-permute-start(bf16[768,768]{1,0:T(8,128)(2,1)} %collective-permute-done.14), channel_id=1, source_target_pairs={{0,1},{1,0},{2,3},{3,2},{4,5},{5,4},{6,7},{7,6},{8,9},{9,8},{10,11... | collective-permute-start | bytes 3538952 | tf_op jit(solution)/shard_map/ppermute | solution.py:34
  120.3 28.3 %collective-permute-start.7 = (bf16[1,512,768]{2,1,0:T(8,128)(2,1)}, bf16[1,512,768]{2,1,0:T(8,128)(2,1)}, u32[]{:S(2)}, u32[]{:S(2)}) collective-permute-start(bf16[1,512,768]{2,1,0:T(8,128)(2,1)} %slice.154), channel_id=1, source_target_pairs={{0,1},{1,0},{2,3},{3,2},{4,5},{5,4},{6,7},{7,6},{8,9},{9,8},{10,11... | collective-permute-start | bytes 2359304 | tf_op jit(solution)/shard_map/ppermute | solution.py:24
  141.1 13.5 %collective-permute-start.6 = (bf16[1,512,768]{1,2,0:T(8,128)(2,1)}, bf16[1,512,768]{1,2,0:T(8,128)(2,1)}, u32[]{:S(2)}, u32[]{:S(2)}) collective-permute-start(bf16[1,512,768]{1,2,0:T(8,128)(2,1)} %slice.152), channel_id=1, source_target_pairs={{0,1},{1,0},{2,3},{3,2},{4,5},{5,4},{6,7},{7,6},{8,9},{9,8},{10,11... | collective-permute-start | bytes 2359304 | tf_op jit(solution)/shard_map/ppermute | solution.py:24
  268.7 11.0 %copy-start.27 = (bf16[1024,768]{1,0:T(8,128)(2,1)}, bf16[1024,768]{1,0:T(8,128)(2,1)S(1)}, u32[]{:S(2)}) copy-start(bf16[1024,768]{1,0:T(8,128)(2,1)S(1)} %fusion.78) | copy-start | bytes 4718596
  268.7 11.0 %copy-start.26 = (bf16[1024,768]{1,0:T(8,128)(2,1)S(1)}, bf16[1024,768]{1,0:T(8,128)(2,1)}, u32[]{:S(2)}) copy-start(bf16[1024,768]{1,0:T(8,128)(2,1)} %get-tuple-element.238) | copy-start | bytes 4718596
  318.3 16.5 %copy-start.4 = (f32[1024,768]{1,0:T(8,128)}, f32[1024,768]{1,0:T(8,128)S(1)}, u32[]{:S(2)}) copy-start(f32[1024,768]{1,0:T(8,128)S(1)} %get-tuple-element.298) | copy-start | bytes 9437188
  318.4 16.4 %copy-start.14 = (bf16[12,1,1024,64]{2,3,1,0:T(8,128)(2,1)S(1)}, bf16[12,1,1024,64]{2,3,1,0:T(8,128)(2,1)}, u32[]{:S(2)}) copy-start(bf16[12,1,1024,64]{2,3,1,0:T(8,128)(2,1)} %get-tuple-element.128) | copy-start | bytes 4718596
  537.8 10.3 %collective-permute-start.29 = (bf16[2,192,768]{2,1,0:T(8,128)(2,1)S(1)}, bf16[2,192,768]{2,1,0:T(8,128)(2,1)S(1)}, u32[]{:S(2)}, u32[]{:S(2)}) collective-permute-start(bf16[2,192,768]{2,1,0:T(8,128)(2,1)S(1)} %dynamic-slice_bitcast_fusion.12), channel_id=1, source_target_pairs={{0,1},{1,0},{2,3},{3,2},{4,5},{5,4},{6,7},{7,6},{8,9},{9,8},{10,11... | collective-permute-start | bytes 1769480 | tf_op jit(solution)/shard_map/ppermute | solution.py:34
  546.2 20.7 %copy-start.16 = (bf16[768,3072]{1,0:T(8,128)(2,1)}, bf16[768,3072]{1,0:T(8,128)(2,1)S(1)}, u32[]{:S(2)}) copy-start(bf16[768,3072]{1,0:T(8,128)(2,1)S(1)} %convolution_convert_fusion.2) | copy-start | bytes 14155780
  547.8 98.6 %collective-permute-start.39 = (bf16[2,768,768]{2,1,0:T(8,128)(2,1)}, bf16[2,768,768]{2,1,0:T(8,128)(2,1)}, u32[]{:S(2)}, u32[]{:S(2)}) collective-permute-start(bf16[2,768,768]{2,1,0:T(8,128)(2,1)} %dynamic-slice_bitcast_fusion.8), channel_id=1, source_target_pairs={{0,1},{1,0},{2,3},{3,2},{4,5},{5,4},{6,7},{7,6},{8,9},{9,8},{10,11... | collective-permute-start | bytes 7077896 | tf_op jit(solution)/shard_map/ppermute | solution.py:34
  548.5 11.0 %copy-start.8 = (f32[12,1,1024,64]{2,3,1,0:T(8,128)S(1)}, f32[12,1,1024,64]{2,3,1,0:T(8,128)}, u32[]{:S(2)}) copy-start(f32[12,1,1024,64]{2,3,1,0:T(8,128)} %get-tuple-element.131) | copy-start | bytes 9437188
  548.5 9.2 %collective-permute-start.30 = (bf16[1,192,768]{2,1,0:T(8,128)(2,1)S(1)}, bf16[1,192,768]{2,1,0:T(8,128)(2,1)S(1)}, u32[]{:S(2)}, u32[]{:S(2)}) collective-permute-start(bf16[1,192,768]{2,1,0:T(8,128)(2,1)S(1)} %constant_dynamic-slice_fusion.9), channel_id=1, source_target_pairs={{0,2},{1,3},{2,0},{3,1},{4,6},{5,7},{6,4},{7,5},{8,10},{9,11},{10,... | collective-permute-start | bytes 884744 | tf_op jit(solution)/shard_map/ppermute | solution.py:34
  552.1 24.1 %collective-permute-start.18 = (f32[1,512,768]{1,2,0:T(8,128)S(1)}, f32[1,512,768]{1,2,0:T(8,128)S(1)}, u32[]{:S(2)}, u32[]{:S(2)}) collective-permute-start(f32[1,512,768]{1,2,0:T(8,128)S(1)} %slice_select_fusion), channel_id=1, source_target_pairs={{0,1},{1,0},{2,3},{3,2},{4,5},{5,4},{6,7},{7,6},{8,9},{9,8},{10,11... | collective-permute-start | bytes 4718600 | tf_op jit(solution)/shard_map/ppermute | solution.py:24
  557.9 8.4 collective-permute-start.31
  559.8 19.4 %collective-permute-start.17 = (f32[1,512,768]{1,2,0:T(8,128)S(1)}, f32[1,512,768]{1,2,0:T(8,128)S(1)}, u32[]{:S(2)}, u32[]{:S(2)}) collective-permute-start(f32[1,512,768]{1,2,0:T(8,128)S(1)} %slice_select_fusion.1), channel_id=1, source_target_pairs={{0,1},{1,0},{2,3},{3,2},{4,5},{5,4},{6,7},{7,6},{8,9},{9,8},{10,11... | collective-permute-start | bytes 4718600 | tf_op jit(solution)/shard_map/ppermute | solution.py:24
  566.4 7.5 collective-permute-start.32
  568.4 82.6 %collective-permute-start.34 = (bf16[2,192,3072]{2,1,0:T(8,128)(2,1)}, bf16[2,192,3072]{2,1,0:T(8,128)(2,1)}, u32[]{:S(2)}, u32[]{:S(2)}) collective-permute-start(bf16[2,192,3072]{2,1,0:T(8,128)(2,1)} %dynamic-slice_bitcast_fusion.9), channel_id=1, source_target_pairs={{0,1},{1,0},{2,3},{3,2},{4,5},{5,4},{6,7},{7,6},{8,9},{9,8},{10,11... | collective-permute-start | bytes 7077896 | tf_op jit(solution)/shard_map/ppermute | solution.py:34
  574.7 56.9 %collective-permute-start.33 = (bf16[192,768]{1,0:T(8,128)(2,1)}, bf16[192,768]{1,0:T(8,128)(2,1)}, u32[]{:S(2)}, u32[]{:S(2)}) collective-permute-start(bf16[192,768]{1,0:T(8,128)(2,1)} %add_convert_fusion.16), channel_id=1, source_target_pairs={{0,24},{4,28},{8,16},{12,20},{16,8},{20,12},{24,0},{28,4},{1,25},{... | collective-permute-start | bytes 884744 | tf_op jit(solution)/shard_map/ppermute | solution.py:34
  613.2 1.6 collective-permute-start.19
  615.8 5.4 collective-permute-start.20
  617.2 27.2 %collective-permute-start.44 = (bf16[2,32,4608]{2,1,0:T(8,128)(2,1)}, bf16[2,32,4608]{2,1,0:T(8,128)(2,1)}, u32[]{:S(2)}, u32[]{:S(2)}) collective-permute-start(bf16[2,32,4608]{2,1,0:T(8,128)(2,1)} %dynamic-slice_bitcast_fusion.11), channel_id=1, source_target_pairs={{0,1},{1,0},{2,3},{3,2},{4,5},{5,4},{6,7},{7,6},{8,9},{9,8},{10,11... | collective-permute-start | bytes 1769480 | tf_op jit(solution)/shard_map/ppermute | solution.py:34
  621.2 4.9 collective-permute-start.21
  626.2 5.3 collective-permute-start.22
  628.7 11.3 %copy-start.64 = (s32[144]{0:T(256)S(1)}, s32[144]{0:T(256)}, u32[]{:S(2)}) copy-start(s32[144]{0:T(256)} %eq.77) | copy-start | bytes 1732
  631.5 26.0 %collective-permute-start.24 = (bf16[2,192,2304]{2,1,0:T(8,128)(2,1)}, bf16[2,192,2304]{2,1,0:T(8,128)(2,1)S(1)}, u32[]{:S(2)}, u32[]{:S(2)}) collective-permute-start(bf16[2,192,2304]{2,1,0:T(8,128)(2,1)} %dynamic-slice_bitcast_fusion.10), channel_id=1, source_target_pairs={{0,1},{1,0},{2,3},{3,2},{4,5},{5,4},{6,7},{7,6},{8,9},{9,8},{10,11... | collective-permute-start | bytes 5308424 | tf_op jit(solution)/shard_map/ppermute | solution.py:34
  631.5 8.3 collective-permute-start.23
  645.9 9.9 %collective-permute-start.45 = (bf16[1,32,4608]{2,1,0:T(8,128)(2,1)S(1)}, bf16[1,32,4608]{2,1,0:T(8,128)(2,1)S(1)}, u32[]{:S(2)}, u32[]{:S(2)}) collective-permute-start(bf16[1,32,4608]{2,1,0:T(8,128)(2,1)S(1)} %constant_dynamic-slice_fusion.6), channel_id=1, source_target_pairs={{0,2},{1,3},{2,0},{3,1},{4,6},{5,7},{6,4},{7,5},{8,10},{9,11},{10,... | collective-permute-start | bytes 884744 | tf_op jit(solution)/shard_map/ppermute | solution.py:34
  649.8 31.3 %collective-permute-start.40 = (bf16[1,768,768]{2,1,0:T(8,128)(2,1)S(1)}, bf16[1,768,768]{2,1,0:T(8,128)(2,1)S(1)}, u32[]{:S(2)}, u32[]{:S(2)}) collective-permute-start(bf16[1,768,768]{2,1,0:T(8,128)(2,1)S(1)} %constant_dynamic-slice_fusion.7), channel_id=1, source_target_pairs={{0,2},{1,3},{2,0},{3,1},{4,6},{5,7},{6,4},{7,5},{8,10},{9,11},{10,... | collective-permute-start | bytes 3538952 | tf_op jit(solution)/shard_map/ppermute | solution.py:34
  653.9 52.5 %collective-permute-start.35 = (bf16[1,192,3072]{2,1,0:T(8,128)(2,1)S(1)}, bf16[1,192,3072]{2,1,0:T(8,128)(2,1)S(1)}, u32[]{:S(2)}, u32[]{:S(2)}) collective-permute-start(bf16[1,192,3072]{2,1,0:T(8,128)(2,1)S(1)} %constant_dynamic-slice_fusion.8), channel_id=1, source_target_pairs={{0,2},{1,3},{2,0},{3,1},{4,6},{5,7},{6,4},{7,5},{8,10},{9,11},{10,... | collective-permute-start | bytes 3538952 | tf_op jit(solution)/shard_map/ppermute | solution.py:34
  655.9 52.5 %collective-permute-start.46 = (bf16[32,4608]{1,0:T(8,128)(2,1)S(1)}, bf16[32,4608]{1,0:T(8,128)(2,1)S(1)}, u32[]{:S(2)}, u32[]{:S(2)}) collective-permute-start(bf16[32,4608]{1,0:T(8,128)(2,1)S(1)} %fusion.96), channel_id=1, source_target_pairs={{0,4},{4,0},{8,12},{12,8},{16,20},{20,16},{24,28},{28,24},{1,5},{5... | collective-permute-start | bytes 884744 | tf_op jit(solution)/shard_map/ppermute | solution.py:34
  658.0 64.2 %collective-permute-start.25 = (bf16[1,192,2304]{2,1,0:T(8,128)(2,1)S(1)}, bf16[1,192,2304]{2,1,0:T(8,128)(2,1)S(1)}, u32[]{:S(2)}, u32[]{:S(2)}) collective-permute-start(bf16[1,192,2304]{2,1,0:T(8,128)(2,1)S(1)} %constant_dynamic-slice_fusion.10), channel_id=1, source_target_pairs={{0,2},{1,3},{2,0},{3,1},{4,6},{5,7},{6,4},{7,5},{8,10},{9,11},{10,... | collective-permute-start | bytes 2654216 | tf_op jit(solution)/shard_map/ppermute | solution.py:34
  681.4 42.6 %collective-permute-start.41 = (bf16[768,768]{1,0:T(8,128)(2,1)S(1)}, bf16[768,768]{1,0:T(8,128)(2,1)S(1)}, u32[]{:S(2)}, u32[]{:S(2)}) collective-permute-start(bf16[768,768]{1,0:T(8,128)(2,1)S(1)} %fusion.88), channel_id=1, source_target_pairs={{0,4},{4,0},{8,12},{12,8},{16,20},{20,16},{24,28},{28,24},{1,5},{5... | collective-permute-start | bytes 3538952 | tf_op jit(solution)/shard_map/ppermute | solution.py:34
  706.8 28.2 %collective-permute-start.36 = (bf16[192,3072]{1,0:T(8,128)(2,1)S(1)}, bf16[192,3072]{1,0:T(8,128)(2,1)S(1)}, u32[]{:S(2)}, u32[]{:S(2)}) collective-permute-start(bf16[192,3072]{1,0:T(8,128)(2,1)S(1)} %fusion.87), channel_id=1, source_target_pairs={{0,4},{4,0},{8,12},{12,8},{16,20},{20,16},{24,28},{28,24},{1,5},{5... | collective-permute-start | bytes 3538952 | tf_op jit(solution)/shard_map/ppermute | solution.py:34
  708.5 29.2 %collective-permute-start.47 = (bf16[32,4608]{1,0:T(8,128)(2,1)S(1)}, bf16[32,4608]{1,0:T(8,128)(2,1)S(1)}, u32[]{:S(2)}, u32[]{:S(2)}) collective-permute-start(bf16[32,4608]{1,0:T(8,128)(2,1)S(1)} %add_convert_fusion.14), channel_id=1, source_target_pairs={{0,8},{4,12},{8,0},{12,4},{16,24},{20,28},{24,16},{28,20},{1,9},{5... | collective-permute-start | bytes 884744 | tf_op jit(solution)/shard_map/ppermute | solution.py:34
  722.4 25.1 %collective-permute-start.26 = (bf16[192,2304]{1,0:T(8,128)(2,1)S(1)}, bf16[192,2304]{1,0:T(8,128)(2,1)S(1)}, u32[]{:S(2)}, u32[]{:S(2)}) collective-permute-start(bf16[192,2304]{1,0:T(8,128)(2,1)S(1)} %fusion.91), channel_id=1, source_target_pairs={{0,4},{4,0},{8,12},{12,8},{16,20},{20,16},{24,28},{28,24},{1,5},{5... | collective-permute-start | bytes 2654216 | tf_op jit(solution)/shard_map/ppermute | solution.py:34
  724.3 30.2 %collective-permute-start.42 = (bf16[768,768]{1,0:T(8,128)(2,1)S(1)}, bf16[768,768]{1,0:T(8,128)(2,1)S(1)}, u32[]{:S(2)}, u32[]{:S(2)}) collective-permute-start(bf16[768,768]{1,0:T(8,128)(2,1)S(1)} %add_convert_fusion.1), channel_id=1, source_target_pairs={{0,8},{4,12},{8,0},{12,4},{16,24},{20,28},{24,16},{28,20},{1,9},{5... | collective-permute-start | bytes 3538952 | tf_op jit(solution)/shard_map/ppermute | solution.py:34
  735.4 49.8 %collective-permute-start.37 = (bf16[192,3072]{1,0:T(8,128)(2,1)S(1)}, bf16[192,3072]{1,0:T(8,128)(2,1)S(1)}, u32[]{:S(2)}, u32[]{:S(2)}) collective-permute-start(bf16[192,3072]{1,0:T(8,128)(2,1)S(1)} %add_convert_fusion.4), channel_id=1, source_target_pairs={{0,8},{4,12},{8,0},{12,4},{16,24},{20,28},{24,16},{28,20},{1,9},{5... | collective-permute-start | bytes 3538952 | tf_op jit(solution)/shard_map/ppermute | solution.py:34
  737.7 68.8 %collective-permute-start.48 = (bf16[32,4608]{1,0:T(8,128)(2,1)S(1)}, bf16[32,4608]{1,0:T(8,128)(2,1)S(1)}, u32[]{:S(2)}, u32[]{:S(2)}) collective-permute-start(bf16[32,4608]{1,0:T(8,128)(2,1)S(1)} %add_convert_fusion.13), channel_id=1, source_target_pairs={{0,24},{4,28},{8,16},{12,20},{16,8},{20,12},{24,0},{28,4},{1,25},{... | collective-permute-start | bytes 884744 | tf_op jit(solution)/shard_map/ppermute | solution.py:34
  747.7 57.4 %collective-permute-start.27 = (bf16[192,2304]{1,0:T(8,128)(2,1)S(1)}, bf16[192,2304]{1,0:T(8,128)(2,1)S(1)}, u32[]{:S(2)}, u32[]{:S(2)}) collective-permute-start(bf16[192,2304]{1,0:T(8,128)(2,1)S(1)} %add_convert_fusion.7), channel_id=1, source_target_pairs={{0,8},{4,12},{8,0},{12,4},{16,24},{20,28},{24,16},{28,20},{1,9},{5... | collective-permute-start | bytes 2654216 | tf_op jit(solution)/shard_map/ppermute | solution.py:34
  754.9 145.0 %collective-permute-start.43 = (bf16[768,768]{1,0:T(8,128)(2,1)S(1)}, bf16[768,768]{1,0:T(8,128)(2,1)S(1)}, u32[]{:S(2)}, u32[]{:S(2)}) collective-permute-start(bf16[768,768]{1,0:T(8,128)(2,1)S(1)} %add_convert_fusion), channel_id=1, source_target_pairs={{0,24},{4,28},{8,16},{12,20},{16,8},{20,12},{24,0},{28,4},{1,25},{... | collective-permute-start | bytes 3538952 | tf_op jit(solution)/shard_map/ppermute | solution.py:34
  785.6 115.9 %collective-permute-start.38 = (bf16[192,3072]{1,0:T(8,128)(2,1)S(1)}, bf16[192,3072]{1,0:T(8,128)(2,1)S(1)}, u32[]{:S(2)}, u32[]{:S(2)}) collective-permute-start(bf16[192,3072]{1,0:T(8,128)(2,1)S(1)} %add_convert_fusion.3), channel_id=1, source_target_pairs={{0,24},{4,28},{8,16},{12,20},{16,8},{20,12},{24,0},{28,4},{1,25},{... | collective-permute-start | bytes 3538952 | tf_op jit(solution)/shard_map/ppermute | solution.py:34
  805.4 93.1 %collective-permute-start.28 = (bf16[192,2304]{1,0:T(8,128)(2,1)S(1)}, bf16[192,2304]{1,0:T(8,128)(2,1)S(1)}, u32[]{:S(2)}, u32[]{:S(2)}) collective-permute-start(bf16[192,2304]{1,0:T(8,128)(2,1)S(1)} %add_convert_fusion.6), channel_id=1, source_target_pairs={{0,24},{4,28},{8,16},{12,20},{16,8},{20,12},{24,0},{28,4},{1,25},{... | collective-permute-start | bytes 2654216 | tf_op jit(solution)/shard_map/ppermute | solution.py:34
  (57 other events, 256.3 us)

commit v2 on v1

--- a/solution.py
+++ b/solution.py
@@ -3,6 +3,8 @@
 import jax
 import jax.numpy as jnp
 from jax import lax
+from jax.experimental import pallas as pl
+from jax.experimental.pallas import tpu as pltpu
 from jax.sharding import PartitionSpec as P
 
 D = 768
@@ -15,7 +17,6 @@
 
 
 eps_norm = 1e-06
-neg_large = -1e30
 
 
 def partner(value, axis, apart):
@@ -120,115 +121,142 @@
     )
 
 
-def split_heads(values):
-    groups = values.shape[0] // PROMPT
-    return values.reshape(groups, PROMPT, HEADS, HDIM).transpose(2, 0, 1, 3)
-
-
-def merge_heads(values):
-    groups = values.shape[1]
-    return values.transpose(1, 2, 0, 3).reshape(groups * PROMPT, HEADS * HDIM)
-
-
-def blocks(values):
-    return values.reshape(values.shape[0], CONTS, CLEN, HDIM)
-
-
-def own_allowed():
-    return (jnp.arange(CONTS, dtype=jnp.int32) >= CONTS // 2)[None, :, None, None]
-
-
-def head_forward(operands):
-    queries, key_main, value_main, key_own, value_own = operands
-    scaling = HDIM ** (-0.5)
-    query_blk = blocks(queries)
-    score_main = (
-        jnp.einsum("gcqd,gkd->gcqk", query_blk, key_main, preferred_element_type=jnp.float32)
-        * scaling
-    )
-    score_own = (
-        jnp.einsum(
-            "gcqd,gckd->gcqk", query_blk, blocks(key_own), preferred_element_type=jnp.float32
-        )
-        * scaling
-    )
-    score_own = jnp.where(own_allowed(), score_own, neg_large)
-    row_max = jnp.maximum(jnp.max(score_main, -1), jnp.max(score_own, -1))
-    denom_sum = jnp.sum(jnp.exp(score_main - row_max[..., None]), -1) + jnp.sum(
-        jnp.exp(score_own - row_max[..., None]), -1
-    )
-    log_sum = row_max + jnp.log(denom_sum)
-    prob_main = jnp.exp(score_main - log_sum[..., None]).astype(jnp.bfloat16)
-    prob_own = jnp.exp(score_own - log_sum[..., None]).astype(jnp.bfloat16)
-    output = jnp.einsum("gcqk,gkd->gcqd", prob_main, value_main, preferred_element_type=jnp.float32)
-    output = output + jnp.einsum(
-        "gcqk,gckd->gcqd", prob_own, blocks(value_own), preferred_element_type=jnp.float32
-    )
-    return (output.reshape(queries.shape[0], PROMPT, HDIM), log_sum)
-
-
-def head_backward(operands):
-    queries, key_main, value_main, key_own, value_own, log_sum, grad_out = operands
-    scaling = HDIM ** (-0.5)
-    groups = queries.shape[0]
-    query_blk = blocks(queries)
-    grad_blk = blocks(grad_out)
-    key_blk = blocks(key_own)
-    score_main = (
-        jnp.einsum("gcqd,gkd->gcqk", query_blk, key_main, preferred_element_type=jnp.float32)
-        * scaling
-    )
-    prob_main = jnp.exp(score_main - log_sum[..., None])
-    score_own = (
-        jnp.einsum("gcqd,gckd->gcqk", query_blk, key_blk, preferred_element_type=jnp.float32)
-        * scaling
-    )
-    score_own = jnp.where(own_allowed(), score_own, neg_large)
-    prob_own = jnp.exp(score_own - log_sum[..., None])
-    grad_prob_main = jnp.einsum(
-        "gcqd,gkd->gcqk", grad_blk, value_main, preferred_element_type=jnp.float32
-    )
-    grad_prob_own = jnp.einsum(
-        "gcqd,gckd->gcqk", grad_blk, blocks(value_own), preferred_element_type=jnp.float32
-    )
-    row_dot = jnp.sum(grad_prob_main * prob_main, -1) + jnp.sum(grad_prob_own * prob_own, -1)
-    grad_value_main = jnp.einsum(
-        "gcqk,gcqd->gkd",
-        prob_main.astype(jnp.bfloat16),
-        grad_blk,
-        preferred_element_type=jnp.float32,
-    )
-    grad_value_own = jnp.einsum(
-        "gcqk,gcqd->gckd",
-        prob_own.astype(jnp.bfloat16),
-        grad_blk,
-        preferred_element_type=jnp.float32,
-    ).reshape(groups, PROMPT, HDIM)
-    grad_score_main = (prob_main * (grad_prob_main - row_dot[..., None])).astype(jnp.bfloat16)
-    grad_score_own = (prob_own * (grad_prob_own - row_dot[..., None])).astype(jnp.bfloat16)
-    grad_query = jnp.einsum(
-        "gcqk,gkd->gcqd", grad_score_main, key_main, preferred_element_type=jnp.float32
-    )
-    grad_query = grad_query + jnp.einsum(
-        "gcqk,gckd->gcqd", grad_score_own, key_blk, preferred_element_type=jnp.float32
-    )
-    grad_key_main = (
-        jnp.einsum("gcqk,gcqd->gkd", grad_score_main, query_blk, preferred_element_type=jnp.float32)
-        * scaling
-    )
-    grad_key_own = (
-        jnp.einsum(
-            "gcqk,gcqd->gckd", grad_score_own, query_blk, preferred_element_type=jnp.float32
-        ).reshape(groups, PROMPT, HDIM)
-        * scaling
-    )
-    return (
-        (grad_query * scaling).reshape(groups, PROMPT, HDIM),
-        grad_key_main,
-        grad_value_main,
-        grad_key_own,
-        grad_value_own,
-    )
+def nt(left, right):
+    return lax.dot_general(left, right, (((1,), (1,)), ((), ())), preferred_element_type=jnp.float32)
+
+
+def nn(left, right):
+    return lax.dot_general(left, right, (((1,), (0,)), ((), ())), preferred_element_type=jnp.float32)
+
+
+def head_only(values, head):
+    lane = lax.broadcasted_iota(jnp.int32, values.shape, 1)
+    return jnp.where((lane < HDIM) if head == 0 else (lane >= HDIM), values, jnp.zeros_like(values))
+
+
+HALF = PROMPT // 2
+TILE = HALF
+PAIRS = HEADS // 2
+
+
+def attn_fwd_kernel(q_ref, k_ref, v_ref, kr_ref, vr_ref, o_ref, lse_ref):
+    k_own, kr = k_ref[...], kr_ref[...]
+    v_own_t, vr_t = v_ref[...].T, vr_ref[...].T
+    for start in range(0, PROMPT, TILE):
+        outs = []
+        q_tile = q_ref[pl.ds(start, TILE), :]
+        cols = [slice(c, c + CLEN) for c in range(0, TILE, CLEN)]
+        rows = [slice(start + c, start + c + CLEN) for c in range(0, TILE, CLEN)]
+        for head in range(2):
+            q_head = head_only(q_tile, head)
+            lanes = slice(HDIM * head, HDIM * (head + 1))
+            keys = [(nt(k_own[:HALF], q_head)), nt(kr, q_head)]
+            if start >= HALF:
+                keys.append(jnp.concatenate([nt(k_own[r], q_head[c]) for r, c in zip(rows, cols)], 1))
+            top = jnp.max(keys[0], 0, keepdims=True)
+            for part in keys[1:]:
+                top = jnp.maximum(top, jnp.max(part, 0, keepdims=True))
+            powers = [jnp.exp(part - top) for part in keys]
+            total = jnp.sum(powers[0], 0, keepdims=True)
+            for part in powers[1:]:
+                total = total + jnp.sum(part, 0, keepdims=True)
+            lse_ref[0, pl.ds(head, 1), pl.ds(start, TILE)] = top + jnp.log(total)
+            scale = 1.0 / total
+            probs = [(part * scale).astype(jnp.bfloat16) for part in powers]
+            out = nn(v_own_t[lanes, :HALF], probs[0]) + nn(vr_t[lanes], probs[1])
+            if start >= HALF:
+                out = out + jnp.concatenate(
+                    [nn(v_own_t[lanes, r], probs[2][:, c]) for r, c in zip(rows, cols)], 1
+                )
+            outs.append(out)
+        o_ref[pl.ds(start, TILE), :] = jnp.concatenate(outs, 0).T.astype(jnp.bfloat16)
+
+
+def attn_bwd_kernel(
+    q_ref, k_ref, v_ref, kr_ref, vr_ref, g_ref, lse_ref, dq_ref, dk_ref, dv_ref, dkr_ref, dvr_ref
+):
+    k_own, v_own, kr, vr = k_ref[...], v_ref[...], kr_ref[...], vr_ref[...]
+    k_own_t, kr_t = k_own.T, kr.T
+    first = lax.broadcasted_iota(jnp.int32, (HALF, 2 * HDIM), 1) < HDIM
+    for start in range(0, PROMPT, TILE):
+        tile = pl.ds(start, TILE)
+        q_tile, g_tile = q_ref[tile, :], g_ref[tile, :]
+        cols = [slice(c, c + CLEN) for c in range(0, TILE, CLEN)]
+        rows = [slice(start + c, start + c + CLEN) for c in range(0, TILE, CLEN)]
+        dqs, dks, dvs = [], [], []
+        for head in range(2):
+            q_head, g_head = head_only(q_tile, head), head_only(g_tile, head)
+            lanes = slice(HDIM * head, HDIM * (head + 1))
+            scores = [nt(k_own[:HALF], q_head), nt(kr, q_head)]
+            dps = [nt(v_own[:HALF], g_head), nt(vr, g_head)]
+            if start >= HALF:
+                scores.append(jnp.concatenate([nt(k_own[r], q_head[c]) for r, c in zip(rows, cols)], 1))
+                dps.append(jnp.concatenate([nt(v_own[r], g_head[c]) for r, c in zip(rows, cols)], 1))
+            lse = lse_ref[0, pl.ds(head, 1), tile]
+            probs = [jnp.exp(part - lse) for part in scores]
+            row_dot = jnp.sum(probs[0] * dps[0], 0, keepdims=True)
+            for p_part, d_part in zip(probs[1:], dps[1:]):
+                row_dot = row_dot + jnp.sum(p_part * d_part, 0, keepdims=True)
+            ds = [(p * (d - row_dot)).astype(jnp.bfloat16) for p, d in zip(probs, dps)]
+            probs = [p.astype(jnp.bfloat16) for p in probs]
+            dq = nn(k_own_t[lanes, :HALF], ds[0]) + nn(kr_t[lanes], ds[1])
+            dk = [nn(ds[0], q_tile), nn(ds[1], q_tile)]
+            dv = [nn(probs[0], g_tile), nn(probs[1], g_tile)]
+            if start >= HALF:
+                dq = dq + jnp.concatenate(
+                    [nn(k_own_t[lanes, r], ds[2][:, c]) for r, c in zip(rows, cols)], 1
+                )
+                dk.append(jnp.concatenate([nn(ds[2][:, c], q_tile[c]) for c in cols], 0))
+                dv.append(jnp.concatenate([nn(probs[2][:, c], g_tile[c]) for c in cols], 0))
+            dqs.append(dq)
+            dks.append(dk)
+            dvs.append(dv)
+        dq_ref[tile, :] = jnp.concatenate(dqs, 0).T * HDIM**-0.5
+        for own_ref, other_ref, parts in ((dk_ref, dkr_ref, dks), (dv_ref, dvr_ref, dvs)):
+            merged = [jnp.where(first, a, b) for a, b in zip(*parts)]
+            if start == 0:
+                own_ref[pl.ds(0, HALF), :] = merged[0]
+                other_ref[...] = merged[1]
+            else:
+                own_ref[pl.ds(0, HALF), :] += merged[0]
+                other_ref[...] += merged[1]
+                own_ref[tile, :] = merged[2]
+
+
+VMEM_LIMIT = 60 * 2**20
+
+
+def lane_block(rows):
+    return pl.BlockSpec((rows, 2 * HDIM), lambda pair: (0, pair))
+
+
+def attn_fwd(q, k, v, kr, vr):
+    return pl.pallas_call(
+        attn_fwd_kernel,
+        grid=(PAIRS,),
+        in_specs=[lane_block(PROMPT)] * 3 + [lane_block(HALF)] * 2,
+        out_specs=[lane_block(PROMPT), pl.BlockSpec((1, 2, PROMPT), lambda pair: (pair, 0, 0))],
+        out_shape=[
+            jax.ShapeDtypeStruct((PROMPT, D), jnp.bfloat16),
+            jax.ShapeDtypeStruct((PAIRS, 2, PROMPT), jnp.float32),
+        ],
+        compiler_params=pltpu.CompilerParams(vmem_limit_bytes=VMEM_LIMIT),
+        cost_estimate=pl.CostEstimate(flops=12 * 10**9, bytes_accessed=10 * 2**20, transcendentals=14 * 10**6),
+    )(q, k, v, kr, vr)
+
+
+def attn_bwd(q, k, v, kr, vr, g, lse):
+    return pl.pallas_call(
+        attn_bwd_kernel,
+        grid=(PAIRS,),
+        in_specs=[lane_block(PROMPT)] * 3
+        + [lane_block(HALF)] * 2
+        + [lane_block(PROMPT), pl.BlockSpec((1, 2, PROMPT), lambda pair: (pair, 0, 0))],
+        out_specs=[lane_block(PROMPT)] * 3 + [lane_block(HALF)] * 2,
+        out_shape=[jax.ShapeDtypeStruct((n, D), jnp.float32) for n in (PROMPT, PROMPT, PROMPT, HALF, HALF)],
+        compiler_params=pltpu.CompilerParams(vmem_limit_bytes=VMEM_LIMIT),
+        cost_estimate=pl.CostEstimate(flops=30 * 10**9, bytes_accessed=24 * 2**20, transcendentals=14 * 10**6),
+    )(q, k, v, kr, vr, g, lse)
 
 
 def on_device(
@@ -268,7 +296,6 @@
     shard_index = lax.axis_index("shard")
     rep_index = lax.axis_index("rep")
     half_index = shard_index % 2
-    is_first = half_index == 0
     pair_index = (rep_index * lax.axis_size("shard") + shard_index) // 2
     tok_count = hidden_in.shape[0]
     groups = tok_count // PROMPT
@@ -315,37 +342,17 @@
     sine_val = jnp.sin(angles)[:, None, :]
     queries = (
         rotary(qkv[:, :D].reshape(tok_count, HEADS, HDIM), cosine, sine_val)
-        .astype(jnp.bfloat16)
         .reshape(tok_count, D)
     )
+    queries = (queries * HDIM**-0.5).astype(jnp.bfloat16)
     keys_low = (
         rotary(qkv[:, D : 2 * D].reshape(tok_count, HEADS, HDIM), cosine, sine_val)
         .astype(jnp.bfloat16)
         .reshape(tok_count, D)
     )
     values_low = qkv[:, 2 * D :].astype(jnp.bfloat16)
-    own_keys = keys_low.reshape(groups, PROMPT, D)[:, :half_len]
-    own_values = values_low.reshape(groups, PROMPT, D)[:, :half_len]
-    received = partner((own_keys, own_values), "shard", 0)
-    key_main = jnp.where(
-        is_first,
-        jnp.concatenate([own_keys, received[0]], 1),
-        jnp.concatenate([received[0], own_keys], 1),
-    ).reshape(tok_count, D)
-    value_main = jnp.where(
-        is_first,
-        jnp.concatenate([own_values, received[1]], 1),
-        jnp.concatenate([received[1], own_values], 1),
-    ).reshape(tok_count, D)
-    operands = (
-        split_heads(queries),
-        split_heads(key_main),
-        split_heads(value_main),
-        split_heads(keys_low),
-        split_heads(values_low),
-    )
-    attn_out, log_sum = lax.map(head_forward, operands)
-    attn_low = merge_heads(attn_out).astype(jnp.bfloat16)
+    received = partner((keys_low[:half_len], values_low[:half_len]), "shard", 0)
+    attn_low, log_sum = attn_fwd(queries, keys_low, values_low, received[0], received[1])
     attn_proj = product(attn_low, proj_mat).reshape(shape_four)
     middle = start + gate_attn * attn_proj
     normed_mlp, inv_mlp = layer_norm(middle)
@@ -380,26 +387,14 @@
     grad_att = (gate_attn * grad_middle).astype(jnp.bfloat16).reshape(tok_count, D)
     grad_proj = contract(attn_low, grad_att)
     grad_attn_o = times_trans(grad_att, proj_back).astype(jnp.bfloat16)
-    back_ops = operands + (log_sum, split_heads(grad_attn_o))
-    grad_queries, grad_key_main, grad_value_main, grad_key_own, grad_value_own = lax.map(
-        head_backward, back_ops
-    )
-    key_main_grp = merge_heads(grad_key_main).reshape(groups, PROMPT, D)
-    value_main_grp = merge_heads(grad_value_main).reshape(groups, PROMPT, D)
-    mine_keys = jnp.where(is_first, key_main_grp[:, :half_len], key_main_grp[:, half_len:])
-    other_keys = jnp.where(is_first, key_main_grp[:, half_len:], key_main_grp[:, :half_len])
-    mine_values = jnp.where(is_first, value_main_grp[:, :half_len], value_main_grp[:, half_len:])
-    other_values = jnp.where(is_first, value_main_grp[:, half_len:], value_main_grp[:, :half_len])
+    grad_queries, grad_keys, grad_values, other_keys, other_values = attn_bwd(
+        queries, keys_low, values_low, received[0], received[1], grad_attn_o, log_sum
+    )
     returned = partner((other_keys, other_values), "shard", 0)
-    zero_half = jnp.zeros((groups, half_len, D), jnp.float32)
-    grad_keys = jnp.concatenate([mine_keys + returned[0], zero_half], 1).reshape(
-        tok_count, D
-    ) + merge_heads(grad_key_own)
-    grad_values = jnp.concatenate([mine_values + returned[1], zero_half], 1).reshape(
-        tok_count, D
-    ) + merge_heads(grad_value_own)
+    grad_keys = jnp.concatenate([grad_keys[:half_len] + returned[0], grad_keys[half_len:]], 0)
+    grad_values = jnp.concatenate([grad_values[:half_len] + returned[1], grad_values[half_len:]], 0)
     query_raw = rotary(
-        merge_heads(grad_queries).reshape(tok_count, HEADS, HDIM), cosine, -sine_val
+        grad_queries.reshape(tok_count, HEADS, HDIM), cosine, -sine_val
     ).reshape(tok_count, D)
     key_raw = rotary(grad_keys.reshape(tok_count, HEADS, HDIM), cosine, -sine_val).reshape(
         tok_count, D

time: 912 us -> 696 us (0.76)
  matrix products: 275 us -> 117 us
  local copies, waits for them, and re-layouts: 187 us -> 103 us
  Pallas kernels: 0 us -> 71.2 us
  other arithmetic: 103 us -> 73.4 us
    dot_general x168 -> x0, matrix products: 163 us -> none  [the longest x12 24.9 us: head_backward(): jnp.einsum('gcqd,gkd->gcqk', grad_blk, value_main, preferred_element_type...]
    pallas_call x0 -> x2, Pallas kernels: none -> 71.2 us  [the longest x1 44.4 us: attn_bwd(): pl.pallas_call(attn_bwd_kernel, grid=(PAIRS,), in_specs=[lane_block(PROMP...]
    while x132 -> x0, local copies, waits for them, and re-layouts: 48.3 us -> none
    dynamic_update_slice x48 -> x0, local copies, waits for them, and re-layouts: 34.4 us -> none  [on_device(): attn_out, log_sum = lax.map(head_forward, operands)]
    reduce_sum x24 -> x0, other arithmetic: 11.9 us -> none  [the longest x12 10.9 us: head_forward(): jnp.sum(jnp.exp(score_main - row_max[..., None]), -1)]
    convert_element_type x24 -> x2, other arithmetic: 14.2 us -> 3.64 us  [the longest x1 3.44 us: on_device(): queries = (queries * HDIM ** (-0.5)).astype(jnp.bfloat16)]
    while x4 -> x0, other arithmetic: 10.1 us -> none  [on_device(): attn_out, log_sum = lax.map(head_forward, operands)]
  transfers between devices with their start and end apart: 49 -> 49, of which waited for: 21 -> 20; matrix products, arithmetic and copies ran while one was open for 19% -> 30% of each run, Pallas kernels for 0% -> 6%
where the time goes in v2:
time: 696 us; the launch traced here: 690 us
  waiting for transfers between devices  290 us (42%)
  matrix products  117 us (17%)
  local copies, waits for them, and re-layouts  103 us (15%)
  other arithmetic  73.4 us (11%)
  Pallas kernels  71.2 us (10%)
  starting transfers between devices  33 us (5%)
    ppermute x45, waiting for transfers between devices, swap(): return lax.ppermute(value, axis, pairs)  290 us
    pallas_call x1, Pallas kernels, attn_bwd(): pl.pallas_call(attn_bwd_kernel, grid=(PAIRS,), in_specs=[lane_block(PROMP...  44.4 us
    dot_general x5, matrix products, product(): return jnp.dot(left_mat, right_mat, preferred_element_type=jnp.float32)  41.3 us
    dot_general x4, matrix products, times_trans(): lax.dot_general(left_mat, right_mat, (((1,), (1,)), ((), ())), preferred_...  35.6 us
    dot_general x4, matrix products, contract(): lax.dot_general(left_mat, right_mat, (((0,), (0,)), ((), ())), preferred_...  34.5 us
    ppermute x45, starting transfers between devices, swap(): return lax.ppermute(value, axis, pairs)  31.9 us
    pallas_call x1, Pallas kernels, attn_fwd(): pl.pallas_call(attn_fwd_kernel, grid=(PAIRS,), in_specs=[lane_block(PROMP...  26.8 us
    dynamic_update_slice x19, local copies, waits for them, and re-layouts, gather_rows(): lax.dynamic_update_slice_in_dim(whole, part, (mine ^ offset) * rows, 0)  25.7 us
  transfers between devices with their start and end apart: 49, of which 20 were waited for; matrix products, arithmetic and copies ran while one was open for 30% of the time, Pallas kernels for 6%

profile of v2, /device:TPU:10, one launch (start us, length us, event | category | flops | bytes accessed | tf_op | source)
XLA Modules:
  0.0 689.7 jit_solution(15915865727422329097)
XLA Ops:
  1.4 4.1 concatenate.37
  16.7 2.7 broadcast_in_dim.99
  20.5 2.4 broadcast_in_dim.100
  43.2 2.2 convert_reduce_fusion.1
  48.7 2.2 constant_dynamic-update-slice_fusion.15
  51.1 2.2 constant_dynamic-update-slice_fusion.14
  53.2 19.8 %collective-permute-done.11 = bf16[192,3072]{1,0:T(8,128)(2,1)} collective-permute-done((bf16[192,3072]{1,0:T(8,128)(2,1)}, bf16[192,3072]{1,0:T(8,128)(2,1)}, u32[]{:S(2)}, u32[]{:S(2)}) %collective-permute-start.11) | collective-permute-done | bytes 1179680 | tf_op jit(solution)/shard_map/ppermute | solution.py:35
  73.0 24.4 %collective-permute-done.14 = bf16[768,768]{1,0:T(8,128)(2,1)} collective-permute-done((bf16[768,768]{1,0:T(8,128)(2,1)}, bf16[768,768]{1,0:T(8,128)(2,1)}, u32[]{:S(2)}, u32[]{:S(2)}) %collective-permute-start.14) | collective-permute-done | bytes 1179680 | tf_op jit(solution)/shard_map/ppermute | solution.py:35
  97.4 2.4 constant_dynamic-update-slice_fusion.3
  99.8 2.4 constant_dynamic-update-slice_fusion.2
  102.2 2.5 constant_dynamic-update-slice_fusion.7
  106.8 7.5 %fusion.81 = (bf16[1024,2304]{1,0:T(8,128)(2,1)}, f32[1024,2304]{1,0:T(8,128)S(1)}) fusion(bf16[1024,768]{1,0:T(8,128)(2,1)S(1)} %fusion.13, bf16[768,2304]{1,0:T(8,128)(2,1)} %constant_dynamic-update-slice_fusion.13), kind=kOutput, calls=%fused_computation.250 | convolution fusion | flops 3626237952 | bytes 19267584 | tf_op jit(solution)/shard_map/dot_general | solution.py:109
  114.3 3.1 fusion.79
  117.4 3.5 copy.36
  121.0 2.4 multiply_subtract_fusion
  125.7 2.3 copy.37
  130.6 3.5 copy.35
  134.1 4.2 multiply_subtract_fusion.1
  138.3 2.7 slice.154.v_ref
  141.0 2.6 copy.39.k_ref
  143.6 3.4 fusion.19
  147.0 2.6 copy.38.q_ref
  149.6 2.4 constant_dynamic-update-slice_fusion.1
  152.0 2.4 constant_dynamic-update-slice_fusion.5
  154.4 26.8 %shard_map.263 = (bf16[1024,768]{1,0:T(8,128)(2,1)}, f32[6,2,1024]{2,1,0:T(2,128)}) custom-call(bf16[1024,768]{1,0:T(8,128)(2,1)} %copy.38.q_ref, bf16[1024,768]{1,0:T(8,128)(2,1)} %copy.39.k_ref, bf16[1024,768]{1,0:T(8,128)(2,1)} %slice.154.v_ref, bf16[512,768]{1,0:T(8,128)(2,1)} %collective-permute-done.6.kr_ref, ...), custom_call_target="tpu_custom_call" | custom-call | flops 12000000000 | bytes 10485760 | tf_op jit(solution)/shard_map/pallas_call | solution.py:234
  181.1 5.0 fusion.77
  187.5 11.0 %fusion.83 = f32[1024,3072]{1,0:T(8,128)} fusion(bf16[1024,768]{1,0:T(8,128)(2,1)S(1)} %fusion.18, bf16[768,3072]{1,0:T(8,128)(2,1)} %constant_dynamic-update-slice_fusion.5), kind=kOutput, calls=%fused_computation.252 | convolution fusion | flops 4831838208 | bytes 18874368 | tf_op jit(solution)/shard_map/dot_general | solution.py:109
  198.5 12.3 %convolution_convert_fusion.1 = bf16[3072,768]{1,0:T(8,128)(2,1)} fusion(bf16[1024,768]{1,0:T(8,128)(2,1)S(1)} %copy-done.20, f32[1024,3072]{1,0:T(8,128)} %fusion.83, f32[3072]{0:T(1024)S(1)} %bitcast.257), kind=kOutput, calls=%fused_computation.14 | convolution fusion | flops 4865654784 | bytes 18886656 | tf_op jit(solution)/shard_map/dot_general | solution.py:119
  210.7 16.0 %convert_reduce_fusion = (f32[3072]{0:T(1024)}, bf16[1024,3072]{1,0:T(8,128)(2,1)S(1)}) fusion(f32[1024,3072]{1,0:T(8,128)} %fusion.83, f32[3072]{0:T(1024)S(1)} %bitcast.258, bf16[1024,768]{1,0:T(8,128)(2,1)S(1)} %copy-done.20, bf16[3072,768]{1,0:T(8,128)(2,1)} %constant_dynamic-update-slice_fusion.1), kind=kOutput, calls=%fused_computation.9 | convolution fusion | flops 4904186880 | bytes 25190400 | tf_op jit(solution)/shard_map/dot_general | solution.py:113
  226.7 10.4 %multiply_reduce_fusion.4 = (f32[768]{0:T(1024)S(1)}, f32[1024]{0:T(1024)S(1)}, f32[1024]{0:T(1024)S(1)}, f32[1024,768]{1,0:T(8,128)S(1)}) fusion(f32[1024,768]{1,0:T(8,128)S(1)} %get-tuple-element.49, f32[8,768]{1,0:T(8,128)S(1)} %get-tuple-element.67, f32[1024]{0:T(1024)S(1)} %get-tuple-element.87, f32[1024]{0:T(1024)S(1)} %get-tuple-element.89, ...), kind=kOutput, calls=%fused_computation.54 | convolution fusion | flops 4838913024 | bytes 17348608 | tf_op jit(solution)/shard_map/dot_general | solution.py:113
  237.2 16.3 %fusion.11 = (bf16[1024,768]{1,0:T(8,128)(2,1)S(1)}, f32[1024,768]{1,0:T(8,128)}, bf16[1024,768]{1,0:T(8,128)(2,1)}, f32[1024,768]{1,0:T(8,128)}) fusion(f32[8,768]{1,0:T(8,128)S(1)} %get-tuple-element.70, f32[1024]{0:T(1024)S(1)} %get-tuple-element.85, f32[1024,768]{1,0:T(8,128)S(1)} %get-tuple-element.49, f32[1024]{0:T(1024)S(1)} %get-tuple-element.89, ...), kind=kOutput, calls=%fused_computation.33 | convolution fusion | flops 4875878400 | bytes 34711552 | tf_op jit(solution)/shard_map/dot_general | solution.py:109
  254.9 2.6 convolution_convert_fusion.4.g_ref
  258.9 44.4 %shard_map.264 = (f32[1024,768]{1,0:T(8,128)}, f32[1024,768]{1,0:T(8,128)}, f32[1024,768]{1,0:T(8,128)}, f32[512,768]{1,0:T(8,128)}, f32[512,768]{1,0:T(8,128)}) custom-call(bf16[1024,768]{1,0:T(8,128)(2,1)} %copy.38.q_ref, bf16[1024,768]{1,0:T(8,128)(2,1)} %copy.39.k_ref, bf16[1024,768]{1,0:T(8,128)(2,1)} %slice.154.v_ref, ...), custom_call_target="tpu_custom_call" | custom-call | flops 30000001024 | bytes 25165824 | tf_op jit(solution)/shard_map/pallas_call | solution.py:249
  305.4 8.0 %convolution_convert_fusion.2 = bf16[768,3072]{1,0:T(8,128)(2,1)S(1)} fusion(bf16[1024,768]{1,0:T(8,128)(2,1)} %copy-done.23, bf16[1024,3072]{1,0:T(8,128)(2,1)} %copy-done.57), kind=kOutput, calls=%fused_computation.15 | convolution fusion | flops 4834197504 | bytes 12582912 | tf_op jit(solution)/shard_map/dot_general | solution.py:119
  318.2 4.8 collective-permute-done.31
  325.8 3.5 copy.42
  329.4 2.4 slice.209
  333.7 2.7 collective-permute-start.33
  336.3 2.6 slice_add_fusion
  340.8 4.0 copy.43
  344.8 5.0 subtract_convert_fusion.1
  351.2 2.6 copy.44
  353.8 2.6 pad_maximum_fusion.2
  356.4 2.6 copy.45
  359.0 2.2 add_convert_fusion.9
  362.0 6.6 multiply_reduce_fusion.5
  368.7 12.7 %convolution_convert_fusion.3 = bf16[768,2304]{1,0:T(8,128)(2,1)} fusion(bf16[1024,768]{1,0:T(8,128)(2,1)S(1)} %copy-done.19, bf16[512,768]{1,0:T(8,128)(2,1)S(1)} %copy-done.31, bf16[512,768]{1,0:T(8,128)(2,1)S(1)} %add_convert_fusion.9, bf16[1024,768]{1,0:T(8,128)(2,1)S(1)} %copy-done.22, bf16[1024,768]{1,0:T(8,128)(2,1)S(1)} %copy-done.21), kind=kOutput, calls=%fused_computation.16 | convolution fusion | flops 3644522496 | bytes 9830400 | tf_op jit(solution)/shard_map/dot_general | solution.py:119
  383.4 4.4 multiply_reduce_fusion.1
  389.5 2.9 select_reduce_fusion
  395.2 4.4 collective-permute-done.20
  401.2 2.8 dynamic-slice_bitcast_fusion.2
  411.6 6.1 collective-permute-done.23
  419.1 2.8 fusion.30
  432.8 3.3 fusion.7
  437.3 2.7 fusion.8
  444.8 22.3 %collective-permute-done.40 = bf16[1,768,768]{2,1,0:T(8,128)(2,1)S(1)} collective-permute-done((bf16[1,768,768]{2,1,0:T(8,128)(2,1)S(1)}, bf16[1,768,768]{2,1,0:T(8,128)(2,1)S(1)}, u32[]{:S(2)}, u32[]{:S(2)}) %collective-permute-start.40) | collective-permute-done | bytes 1179680 | tf_op jit(solution)/shard_map/ppermute | solution.py:35
  469.0 23.4 %collective-permute-done.35 = bf16[1,192,3072]{2,1,0:T(8,128)(2,1)S(1)} collective-permute-done((bf16[1,192,3072]{2,1,0:T(8,128)(2,1)S(1)}, bf16[1,192,3072]{2,1,0:T(8,128)(2,1)S(1)}, u32[]{:S(2)}, u32[]{:S(2)}) %collective-permute-start.35) | collective-permute-done | bytes 1179680 | tf_op jit(solution)/shard_map/ppermute | solution.py:35
  495.3 14.8 %collective-permute-done.25 = bf16[1,192,2304]{2,1,0:T(8,128)(2,1)S(1)} collective-permute-done((bf16[1,192,2304]{2,1,0:T(8,128)(2,1)S(1)}, bf16[1,192,2304]{2,1,0:T(8,128)(2,1)S(1)}, u32[]{:S(2)}, u32[]{:S(2)}) %collective-permute-start.25) | collective-permute-done | bytes 884768 | tf_op jit(solution)/shard_map/ppermute | solution.py:35
  513.0 8.8 %collective-permute-done.36 = bf16[192,3072]{1,0:T(8,128)(2,1)S(1)} collective-permute-done((bf16[192,3072]{1,0:T(8,128)(2,1)S(1)}, bf16[192,3072]{1,0:T(8,128)(2,1)S(1)}, u32[]{:S(2)}, u32[]{:S(2)}) %collective-permute-start.36) | collective-permute-done | bytes 1179680 | tf_op jit(solution)/shard_map/ppermute | solution.py:35
  523.5 13.7 %collective-permute-done.26 = bf16[192,2304]{1,0:T(8,128)(2,1)S(1)} collective-permute-done((bf16[192,2304]{1,0:T(8,128)(2,1)S(1)}, bf16[192,2304]{1,0:T(8,128)(2,1)S(1)}, u32[]{:S(2)}, u32[]{:S(2)}) %collective-permute-start.26) | collective-permute-done | bytes 884768 | tf_op jit(solution)/shard_map/ppermute | solution.py:35
  538.2 3.1 collective-permute-done.42
  541.9 28.0 %collective-permute-done.37 = bf16[192,3072]{1,0:T(8,128)(2,1)S(1)} collective-permute-done((bf16[192,3072]{1,0:T(8,128)(2,1)S(1)}, bf16[192,3072]{1,0:T(8,128)(2,1)S(1)}, u32[]{:S(2)}, u32[]{:S(2)}) %collective-permute-start.37) | collective-permute-done | bytes 1179680 | tf_op jit(solution)/shard_map/ppermute | solution.py:35
  570.4 21.4 %collective-permute-done.27 = bf16[192,2304]{1,0:T(8,128)(2,1)S(1)} collective-permute-done((bf16[192,2304]{1,0:T(8,128)(2,1)S(1)}, bf16[192,2304]{1,0:T(8,128)(2,1)S(1)}, u32[]{:S(2)}, u32[]{:S(2)}) %collective-permute-start.27) | collective-permute-done | bytes 884768 | tf_op jit(solution)/shard_map/ppermute | solution.py:35
  593.3 91.4 %collective-permute-done.28 = bf16[192,2304]{1,0:T(8,128)(2,1)S(1)} collective-permute-done((bf16[192,2304]{1,0:T(8,128)(2,1)S(1)}, bf16[192,2304]{1,0:T(8,128)(2,1)S(1)}, u32[]{:S(2)}, u32[]{:S(2)}) %collective-permute-start.28) | collective-permute-done | bytes 884768 | tf_op jit(solution)/shard_map/ppermute | solution.py:35
  (339 shorter events, 114.4 us)
Async XLA Ops:
  0.6 11.3 %copy-start = (f32[1000,128]{1,0:T(8,128)S(1)}, f32[1000,128]{1,0:T(8,128)}, u32[]{:S(2)}) copy-start(f32[1000,128]{1,0:T(8,128)} %param.19) | copy-start | bytes 1536004
  0.7 12.9 %copy-start.29 = (bf16[32,4608]{1,0:T(8,128)(2,1)S(1)}, bf16[32,4608]{1,0:T(8,128)(2,1)}, u32[]{:S(2)}) copy-start(bf16[32,4608]{1,0:T(8,128)(2,1)} %param.24) | copy-start | bytes 884740
  0.7 26.0 %collective-permute-start.9 = (bf16[192,768]{1,0:T(8,128)(2,1)}, bf16[192,768]{1,0:T(8,128)(2,1)}, u32[]{:S(2)}, u32[]{:S(2)}) collective-permute-start(bf16[192,768]{1,0:T(8,128)(2,1)} %param.21), channel_id=1, source_target_pairs={{0,1},{1,0},{2,3},{3,2},{4,5},{5,4},{6,7},{7,6},{8,9},{9,8},{10,11... | collective-permute-start | bytes 884744 | tf_op jit(solution)/shard_map/ppermute | solution.py:35
  0.8 24.1 %collective-permute-start.8 = (bf16[192,768]{1,0:T(8,128)(2,1)}, bf16[192,768]{1,0:T(8,128)(2,1)}, u32[]{:S(2)}, u32[]{:S(2)}) collective-permute-start(bf16[192,768]{1,0:T(8,128)(2,1)} %param.21), channel_id=1, source_target_pairs={{0,2},{1,3},{2,0},{3,1},{4,6},{5,7},{6,4},{7,5},{8,10},{9,11},{10,... | collective-permute-start | bytes 884744 | tf_op jit(solution)/shard_map/ppermute | solution.py:35
  7.2 21.7 %collective-permute-start = (bf16[1,33,4608]{2,1,0:T(8,128)(2,1)}, bf16[1,33,4608]{2,1,0:T(8,128)(2,1)}, u32[]{:S(2)}, u32[]{:S(2)}) collective-permute-start(bf16[1,33,4608]{2,1,0:T(8,128)(2,1)} %maximum_bitcast_fusion), channel_id=1, source_target_pairs={{0,2},{1,3},{2,0},{3,1},{4,6},{5,7},{6,4},{7,5},{8,10},{9,11},{10,... | collective-permute-start | bytes 912392 | tf_op jit(solution)/shard_map/ppermute | solution.py:35
  8.7 21.4 %collective-permute-start.1 = (bf16[1,33,4608]{2,1,0:T(8,128)(2,1)}, bf16[1,33,4608]{2,1,0:T(8,128)(2,1)}, u32[]{:S(2)}, u32[]{:S(2)}) collective-permute-start(bf16[1,33,4608]{2,1,0:T(8,128)(2,1)} %maximum_bitcast_fusion), channel_id=1, source_target_pairs={{0,1},{1,0},{2,3},{3,2},{4,5},{5,4},{6,7},{7,6},{8,9},{9,8},{10,11... | collective-permute-start | bytes 912392 | tf_op jit(solution)/shard_map/ppermute | solution.py:35
  8.7 42.2 %collective-permute-start.4 = (bf16[192,2304]{1,0:T(8,128)(2,1)}, bf16[192,2304]{1,0:T(8,128)(2,1)}, u32[]{:S(2)}, u32[]{:S(2)}) collective-permute-start(bf16[192,2304]{1,0:T(8,128)(2,1)} %param.20), channel_id=1, source_target_pairs={{0,1},{1,0},{2,3},{3,2},{4,5},{5,4},{6,7},{7,6},{8,9},{9,8},{10,11... | collective-permute-start | bytes 2654216 | tf_op jit(solution)/shard_map/ppermute | solution.py:35
  12.2 24.2 %copy-start.37 = (f32[9,128]{1,0:T(8,128)}, f32[9,128]{1,0:T(8,128)S(1)}, u32[]{:S(2)}) copy-start(f32[9,128]{1,0:T(8,128)S(1)} %fusion.40) | copy-start | bytes 13828
  24.8 13.2 %copy-start.55 = (s32[8]{0:T(128)}, s32[8]{0:T(128)S(1)}, u32[]{:S(2)}) copy-start(s32[8]{0:T(128)S(1)} %compare_select_fusion) | copy-start | bytes 100
  24.8 23.5 %collective-permute-start.3 = (bf16[192,2304]{1,0:T(8,128)(2,1)}, bf16[192,2304]{1,0:T(8,128)(2,1)}, u32[]{:S(2)}, u32[]{:S(2)}) collective-permute-start(bf16[192,2304]{1,0:T(8,128)(2,1)} %param.20), channel_id=1, source_target_pairs={{0,2},{1,3},{2,0},{3,1},{4,6},{5,7},{6,4},{7,5},{8,10},{9,11},{10,... | collective-permute-start | bytes 2654216 | tf_op jit(solution)/shard_map/ppermute | solution.py:35
  26.6 46.4 %collective-permute-start.11 = (bf16[192,3072]{1,0:T(8,128)(2,1)}, bf16[192,3072]{1,0:T(8,128)(2,1)}, u32[]{:S(2)}, u32[]{:S(2)}) collective-permute-start(bf16[192,3072]{1,0:T(8,128)(2,1)} %param.22), channel_id=1, source_target_pairs={{0,2},{1,3},{2,0},{3,1},{4,6},{5,7},{6,4},{7,5},{8,10},{9,11},{10,... | collective-permute-start | bytes 3538952 | tf_op jit(solution)/shard_map/ppermute | solution.py:35
  29.0 2.7 collective-permute-start.10
  30.1 2.1 collective-permute-start.2
  31.7 68.1 %collective-permute-start.15 = (bf16[768,768]{1,0:T(8,128)(2,1)}, bf16[768,768]{1,0:T(8,128)(2,1)}, u32[]{:S(2)}, u32[]{:S(2)}) collective-permute-start(bf16[768,768]{1,0:T(8,128)(2,1)} %param.23), channel_id=1, source_target_pairs={{0,1},{1,0},{2,3},{3,2},{4,5},{5,4},{6,7},{7,6},{8,9},{9,8},{10,11... | collective-permute-start | bytes 3538952 | tf_op jit(solution)/shard_map/ppermute | solution.py:35
  32.2 65.2 %collective-permute-start.14 = (bf16[768,768]{1,0:T(8,128)(2,1)}, bf16[768,768]{1,0:T(8,128)(2,1)}, u32[]{:S(2)}, u32[]{:S(2)}) collective-permute-start(bf16[768,768]{1,0:T(8,128)(2,1)} %param.23), channel_id=1, source_target_pairs={{0,2},{1,3},{2,0},{3,1},{4,6},{5,7},{6,4},{7,5},{8,10},{9,11},{10,... | collective-permute-start | bytes 3538952 | tf_op jit(solution)/shard_map/ppermute | solution.py:35
  46.9 59.9 %copy-start.18 = (bf16[1024,768]{1,0:T(8,128)(2,1)}, bf16[1024,768]{1,0:T(8,128)(2,1)S(1)}, u32[]{:S(2)}) copy-start(bf16[1024,768]{1,0:T(8,128)(2,1)S(1)} %fusion.13) | copy-start | bytes 4718596
  48.4 56.3 %collective-permute-start.12 = (bf16[192,3072]{1,0:T(8,128)(2,1)S(1)}, bf16[192,3072]{1,0:T(8,128)(2,1)S(1)}, u32[]{:S(2)}, u32[]{:S(2)}) collective-permute-start(bf16[192,3072]{1,0:T(8,128)(2,1)S(1)} %copy-done.27), channel_id=1, source_target_pairs={{0,1},{1,0},{2,3},{3,2},{4,5},{5,4},{6,7},{7,6},{8,9},{9,8},{10,11... | collective-permute-start | bytes 3538952 | tf_op jit(solution)/shard_map/ppermute | solution.py:35
  50.9 54.8 %collective-permute-start.5 = (bf16[192,2304]{1,0:T(8,128)(2,1)}, bf16[192,2304]{1,0:T(8,128)(2,1)S(1)}, u32[]{:S(2)}, u32[]{:S(2)}) collective-permute-start(bf16[192,2304]{1,0:T(8,128)(2,1)} %collective-permute-done.3), channel_id=1, source_target_pairs={{0,1},{1,0},{2,3},{3,2},{4,5},{5,4},{6,7},{7,6},{8,9},{9,8},{10,11... | collective-permute-start | bytes 2654216 | tf_op jit(solution)/shard_map/ppermute | solution.py:35
  73.0 78.9 %collective-permute-start.13 = (bf16[192,3072]{1,0:T(8,128)(2,1)}, bf16[192,3072]{1,0:T(8,128)(2,1)}, u32[]{:S(2)}, u32[]{:S(2)}) collective-permute-start(bf16[192,3072]{1,0:T(8,128)(2,1)} %collective-permute-done.11), channel_id=1, source_target_pairs={{0,1},{1,0},{2,3},{3,2},{4,5},{5,4},{6,7},{7,6},{8,9},{9,8},{10,11... | collective-permute-start | bytes 3538952 | tf_op jit(solution)/shard_map/ppermute | solution.py:35
  97.4 52.2 %collective-permute-start.16 = (bf16[768,768]{1,0:T(8,128)(2,1)}, bf16[768,768]{1,0:T(8,128)(2,1)}, u32[]{:S(2)}, u32[]{:S(2)}) collective-permute-start(bf16[768,768]{1,0:T(8,128)(2,1)} %collective-permute-done.14), channel_id=1, source_target_pairs={{0,1},{1,0},{2,3},{3,2},{4,5},{5,4},{6,7},{7,6},{8,9},{9,8},{10,11... | collective-permute-start | bytes 3538952 | tf_op jit(solution)/shard_map/ppermute | solution.py:35
  130.0 24.3 %collective-permute-start.7 = (bf16[512,768]{1,0:T(8,128)(2,1)}, bf16[512,768]{1,0:T(8,128)(2,1)}, u32[]{:S(2)}, u32[]{:S(2)}) collective-permute-start(bf16[512,768]{1,0:T(8,128)(2,1)} %slice.156), channel_id=1, source_target_pairs={{0,1},{1,0},{2,3},{3,2},{4,5},{5,4},{6,7},{7,6},{8,9},{9,8},{10,11... | collective-permute-start | bytes 2359304 | tf_op jit(solution)/shard_map/ppermute | solution.py:25
  130.4 24.0 %collective-permute-start.6 = (bf16[512,768]{1,0:T(8,128)(2,1)}, bf16[512,768]{1,0:T(8,128)(2,1)}, u32[]{:S(2)}, u32[]{:S(2)}) collective-permute-start(bf16[512,768]{1,0:T(8,128)(2,1)} %copy.37), channel_id=1, source_target_pairs={{0,1},{1,0},{2,3},{3,2},{4,5},{5,4},{6,7},{7,6},{8,9},{9,8},{10,11... | collective-permute-start | bytes 2359304 | tf_op jit(solution)/shard_map/ppermute | solution.py:25
  187.4 11.0 %copy-start.23 = (bf16[1024,768]{1,0:T(8,128)(2,1)}, bf16[1024,768]{1,0:T(8,128)(2,1)S(1)}, u32[]{:S(2)}) copy-start(bf16[1024,768]{1,0:T(8,128)(2,1)S(1)} %fusion.18) | copy-start | bytes 4718596
  187.4 11.0 %copy-start.20 = (bf16[1024,768]{1,0:T(8,128)(2,1)S(1)}, bf16[1024,768]{1,0:T(8,128)(2,1)}, u32[]{:S(2)}) copy-start(bf16[1024,768]{1,0:T(8,128)(2,1)} %get-tuple-element.45) | copy-start | bytes 4718596
  187.4 11.0 %copy-start.44 = (f32[4,1,768]{2,1,0:T(1,128)S(1)}, f32[4,1,768]{2,1,0:T(1,128)}, u32[]{:S(2)}) copy-start(f32[4,1,768]{2,1,0:T(1,128)} %slice_convert_fusion.2) | copy-start | bytes 36868
  237.1 16.3 %copy-start.3 = (f32[1024,768]{1,0:T(8,128)}, f32[1024,768]{1,0:T(8,128)S(1)}, u32[]{:S(2)}) copy-start(f32[1024,768]{1,0:T(8,128)S(1)} %get-tuple-element.93) | copy-start | bytes 9437188
  237.2 16.3 %copy-start.24 = (bf16[1024,768]{1,0:T(8,128)(2,1)S(1)}, bf16[1024,768]{1,0:T(8,128)(2,1)}, u32[]{:S(2)}) copy-start(bf16[1024,768]{1,0:T(8,128)(2,1)} %get-tuple-element.21) | copy-start | bytes 4718596
  258.4 45.0 %collective-permute-start.29 = (bf16[2,192,768]{2,1,0:T(8,128)(2,1)}, bf16[2,192,768]{2,1,0:T(8,128)(2,1)}, u32[]{:S(2)}, u32[]{:S(2)}) collective-permute-start(bf16[2,192,768]{2,1,0:T(8,128)(2,1)} %dynamic-slice_bitcast_fusion.4), channel_id=1, source_target_pairs={{0,1},{1,0},{2,3},{3,2},{4,5},{5,4},{6,7},{7,6},{8,9},{9,8},{10,11... | collective-permute-start | bytes 1769480 | tf_op jit(solution)/shard_map/ppermute | solution.py:35
  303.3 33.0 %collective-permute-start.17 = (f32[512,768]{1,0:T(8,128)}, f32[512,768]{1,0:T(8,128)}, u32[]{:S(2)}, u32[]{:S(2)}) collective-permute-start(f32[512,768]{1,0:T(8,128)} %get-tuple-element.25), channel_id=1, source_target_pairs={{0,1},{1,0},{2,3},{3,2},{4,5},{5,4},{6,7},{7,6},{8,9},{9,8},{10,11... | collective-permute-start | bytes 4718600 | tf_op jit(solution)/shard_map/ppermute | solution.py:25
  304.8 11.2 %slice-start = ((s8[4718592]{0:T(1024)(128)(4,1)}), s8[4194304]{0:T(1024)(128)(4,1)S(1)}, s32[]{:S(2)}) async-start(s8[4718592]{0:T(1024)(128)(4,1)} %bitcast.243), calls=%async_computation | async-start | bytes 8388608
  304.8 11.1 %slice-start.1 = ((s8[4718592]{0:T(1024)(128)(4,1)}), s8[524288]{0:T(1024)(128)(4,1)S(1)}, s32[]{:S(2)}) async-start(s8[4718592]{0:T(1024)(128)(4,1)} %bitcast.243), calls=%async_computation.1 | async-start | bytes 1048576
  304.8 9.4 %collective-permute-start.30 = (bf16[1,192,768]{2,1,0:T(8,128)(2,1)S(1)}, bf16[1,192,768]{2,1,0:T(8,128)(2,1)S(1)}, u32[]{:S(2)}, u32[]{:S(2)}) collective-permute-start(bf16[1,192,768]{2,1,0:T(8,128)(2,1)S(1)} %constant_dynamic-slice_fusion.9), channel_id=1, source_target_pairs={{0,2},{1,3},{2,0},{3,1},{4,6},{5,7},{6,4},{7,5},{8,10},{9,11},{10,... | collective-permute-start | bytes 884744 | tf_op jit(solution)/shard_map/ppermute | solution.py:35
  314.4 8.7 %collective-permute-start.31 = (bf16[192,768]{1,0:T(8,128)(2,1)S(1)}, bf16[192,768]{1,0:T(8,128)(2,1)S(1)}, u32[]{:S(2)}, u32[]{:S(2)}) collective-permute-start(bf16[192,768]{1,0:T(8,128)(2,1)S(1)} %fusion.31), channel_id=1, source_target_pairs={{0,4},{4,0},{8,12},{12,8},{16,20},{20,16},{24,28},{28,24},{1,5},{5... | collective-permute-start | bytes 884744 | tf_op jit(solution)/shard_map/ppermute | solution.py:35
  317.5 115.3 %collective-permute-start.39 = (bf16[2,768,768]{2,1,0:T(8,128)(2,1)}, bf16[2,768,768]{2,1,0:T(8,128)(2,1)}, u32[]{:S(2)}, u32[]{:S(2)}) collective-permute-start(bf16[2,768,768]{2,1,0:T(8,128)(2,1)} %dynamic-slice_bitcast_fusion), channel_id=1, source_target_pairs={{0,1},{1,0},{2,3},{3,2},{4,5},{5,4},{6,7},{7,6},{8,9},{9,8},{10,11... | collective-permute-start | bytes 7077896 | tf_op jit(solution)/shard_map/ppermute | solution.py:35
  317.5 41.5 %collective-permute-start.18 = (f32[512,768]{1,0:T(8,128)}, f32[512,768]{1,0:T(8,128)}, u32[]{:S(2)}, u32[]{:S(2)}) collective-permute-start(f32[512,768]{1,0:T(8,128)} %get-tuple-element.27), channel_id=1, source_target_pairs={{0,1},{1,0},{2,3},{3,2},{4,5},{5,4},{6,7},{7,6},{8,9},{9,8},{10,11... | collective-permute-start | bytes 4718600 | tf_op jit(solution)/shard_map/ppermute | solution.py:25
  323.8 8.0 %collective-permute-start.32 = (bf16[192,768]{1,0:T(8,128)(2,1)}, bf16[192,768]{1,0:T(8,128)(2,1)}, u32[]{:S(2)}, u32[]{:S(2)}) collective-permute-start(bf16[192,768]{1,0:T(8,128)(2,1)} %add_convert_fusion.16), channel_id=1, source_target_pairs={{0,8},{4,12},{8,0},{12,4},{16,24},{20,28},{24,16},{28,20},{1,9},{5... | collective-permute-start | bytes 884744 | tf_op jit(solution)/shard_map/ppermute | solution.py:35
  325.8 111.4 %collective-permute-start.34 = (bf16[2,192,3072]{2,1,0:T(8,128)(2,1)}, bf16[2,192,3072]{2,1,0:T(8,128)(2,1)}, u32[]{:S(2)}, u32[]{:S(2)}) collective-permute-start(bf16[2,192,3072]{2,1,0:T(8,128)(2,1)} %dynamic-slice_bitcast_fusion.1), channel_id=1, source_target_pairs={{0,1},{1,0},{2,3},{3,2},{4,5},{5,4},{6,7},{7,6},{8,9},{9,8},{10,11... | collective-permute-start | bytes 7077896 | tf_op jit(solution)/shard_map/ppermute | solution.py:35
  333.7 75.8 %collective-permute-start.33 = (bf16[192,768]{1,0:T(8,128)(2,1)}, bf16[192,768]{1,0:T(8,128)(2,1)}, u32[]{:S(2)}, u32[]{:S(2)}) collective-permute-start(bf16[192,768]{1,0:T(8,128)(2,1)} %add_convert_fusion.15), channel_id=1, source_target_pairs={{0,24},{4,28},{8,16},{12,20},{16,8},{20,12},{24,0},{28,4},{1,25},{... | collective-permute-start | bytes 884744 | tf_op jit(solution)/shard_map/ppermute | solution.py:35
  368.7 13.0 %copy-start.8 = (f32[1024,768]{1,0:T(8,128)S(1)}, f32[1024,768]{1,0:T(8,128)}, u32[]{:S(2)}) copy-start(f32[1024,768]{1,0:T(8,128)} %get-tuple-element.94) | copy-start | bytes 9437188
  368.7 13.0 %copy-start.10 = (f32[1024,768]{1,0:T(8,128)S(1)}, f32[1024,768]{1,0:T(8,128)}, u32[]{:S(2)}) copy-start(f32[1024,768]{1,0:T(8,128)} %get-tuple-element.92) | copy-start | bytes 9437188
  392.6 1.4 collective-permute-start.19
  394.1 11.9 %copy-start.9 = (f32[1024,768]{1,0:T(8,128)S(1)}, f32[1024,768]{1,0:T(8,128)}, u32[]{:S(2)}) copy-start(f32[1024,768]{1,0:T(8,128)} %get-tuple-element.43) | copy-start | bytes 9437188
  394.1 5.5 collective-permute-start.20
  395.1 35.4 %collective-permute-start.44 = (bf16[2,32,4608]{2,1,0:T(8,128)(2,1)S(1)}, bf16[2,32,4608]{2,1,0:T(8,128)(2,1)}, u32[]{:S(2)}, u32[]{:S(2)}) collective-permute-start(bf16[2,32,4608]{2,1,0:T(8,128)(2,1)S(1)} %dynamic-slice_bitcast_fusion.3), channel_id=1, source_target_pairs={{0,1},{1,0},{2,3},{3,2},{4,5},{5,4},{6,7},{7,6},{8,9},{9,8},{10,11... | collective-permute-start | bytes 1769480 | tf_op jit(solution)/shard_map/ppermute | solution.py:35
  399.6 4.9 collective-permute-start.21
  404.5 4.9 collective-permute-start.22
  409.4 34.0 %collective-permute-start.24 = (bf16[2,192,2304]{2,1,0:T(8,128)(2,1)}, bf16[2,192,2304]{2,1,0:T(8,128)(2,1)S(1)}, u32[]{:S(2)}, u32[]{:S(2)}) collective-permute-start(bf16[2,192,2304]{2,1,0:T(8,128)(2,1)} %dynamic-slice_bitcast_fusion.2), channel_id=1, source_target_pairs={{0,1},{1,0},{2,3},{3,2},{4,5},{5,4},{6,7},{7,6},{8,9},{9,8},{10,11... | collective-permute-start | bytes 5308424 | tf_op jit(solution)/shard_map/ppermute | solution.py:35
  409.5 8.3 %collective-permute-start.23 = (f32[228,128]{1,0:T(8,128)S(1)}, f32[228,128]{1,0:T(8,128)S(1)}, u32[]{:S(2)}, u32[]{:S(2)}) collective-permute-start(f32[228,128]{1,0:T(8,128)S(1)} %add.519), channel_id=1, source_target_pairs={{0,24},{4,28},{8,16},{12,20},{16,8},{20,12},{24,0},{28,4},{1,25},{... | collective-permute-start | bytes 350216 | tf_op jit(solution)/shard_map/ppermute | solution.py:35
  431.8 10.0 %collective-permute-start.45 = (bf16[1,32,4608]{2,1,0:T(8,128)(2,1)S(1)}, bf16[1,32,4608]{2,1,0:T(8,128)(2,1)S(1)}, u32[]{:S(2)}, u32[]{:S(2)}) collective-permute-start(bf16[1,32,4608]{2,1,0:T(8,128)(2,1)S(1)} %constant_dynamic-slice_fusion.6), channel_id=1, source_target_pairs={{0,2},{1,3},{2,0},{3,1},{4,6},{5,7},{6,4},{7,5},{8,10},{9,11},{10,... | collective-permute-start | bytes 884744 | tf_op jit(solution)/shard_map/ppermute | solution.py:35
  436.2 30.9 %collective-permute-start.40 = (bf16[1,768,768]{2,1,0:T(8,128)(2,1)S(1)}, bf16[1,768,768]{2,1,0:T(8,128)(2,1)S(1)}, u32[]{:S(2)}, u32[]{:S(2)}) collective-permute-start(bf16[1,768,768]{2,1,0:T(8,128)(2,1)S(1)} %constant_dynamic-slice_fusion.7), channel_id=1, source_target_pairs={{0,2},{1,3},{2,0},{3,1},{4,6},{5,7},{6,4},{7,5},{8,10},{9,11},{10,... | collective-permute-start | bytes 3538952 | tf_op jit(solution)/shard_map/ppermute | solution.py:35
  440.1 52.3 %collective-permute-start.35 = (bf16[1,192,3072]{2,1,0:T(8,128)(2,1)S(1)}, bf16[1,192,3072]{2,1,0:T(8,128)(2,1)S(1)}, u32[]{:S(2)}, u32[]{:S(2)}) collective-permute-start(bf16[1,192,3072]{2,1,0:T(8,128)(2,1)S(1)} %constant_dynamic-slice_fusion.8), channel_id=1, source_target_pairs={{0,2},{1,3},{2,0},{3,1},{4,6},{5,7},{6,4},{7,5},{8,10},{9,11},{10,... | collective-permute-start | bytes 3538952 | tf_op jit(solution)/shard_map/ppermute | solution.py:35
  441.9 52.5 %collective-permute-start.46 = (bf16[32,4608]{1,0:T(8,128)(2,1)S(1)}, bf16[32,4608]{1,0:T(8,128)(2,1)S(1)}, u32[]{:S(2)}, u32[]{:S(2)}) collective-permute-start(bf16[32,4608]{1,0:T(8,128)(2,1)S(1)} %fusion.32), channel_id=1, source_target_pairs={{0,4},{4,0},{8,12},{12,8},{16,20},{20,16},{24,28},{28,24},{1,5},{5... | collective-permute-start | bytes 884744 | tf_op jit(solution)/shard_map/ppermute | solution.py:35
  444.0 66.1 %collective-permute-start.25 = (bf16[1,192,2304]{2,1,0:T(8,128)(2,1)S(1)}, bf16[1,192,2304]{2,1,0:T(8,128)(2,1)S(1)}, u32[]{:S(2)}, u32[]{:S(2)}) collective-permute-start(bf16[1,192,2304]{2,1,0:T(8,128)(2,1)S(1)} %constant_dynamic-slice_fusion.10), channel_id=1, source_target_pairs={{0,2},{1,3},{2,0},{3,1},{4,6},{5,7},{6,4},{7,5},{8,10},{9,11},{10,... | collective-permute-start | bytes 2654216 | tf_op jit(solution)/shard_map/ppermute | solution.py:35
  467.4 44.5 %collective-permute-start.41 = (bf16[768,768]{1,0:T(8,128)(2,1)S(1)}, bf16[768,768]{1,0:T(8,128)(2,1)S(1)}, u32[]{:S(2)}, u32[]{:S(2)}) collective-permute-start(bf16[768,768]{1,0:T(8,128)(2,1)S(1)} %fusion.25), channel_id=1, source_target_pairs={{0,4},{4,0},{8,12},{12,8},{16,20},{20,16},{24,28},{28,24},{1,5},{5... | collective-permute-start | bytes 3538952 | tf_op jit(solution)/shard_map/ppermute | solution.py:35
  492.8 29.0 %collective-permute-start.36 = (bf16[192,3072]{1,0:T(8,128)(2,1)S(1)}, bf16[192,3072]{1,0:T(8,128)(2,1)S(1)}, u32[]{:S(2)}, u32[]{:S(2)}) collective-permute-start(bf16[192,3072]{1,0:T(8,128)(2,1)S(1)} %fusion.24), channel_id=1, source_target_pairs={{0,4},{4,0},{8,12},{12,8},{16,20},{20,16},{24,28},{28,24},{1,5},{5... | collective-permute-start | bytes 3538952 | tf_op jit(solution)/shard_map/ppermute | solution.py:35
  494.5 28.5 %collective-permute-start.47 = (bf16[32,4608]{1,0:T(8,128)(2,1)S(1)}, bf16[32,4608]{1,0:T(8,128)(2,1)S(1)}, u32[]{:S(2)}, u32[]{:S(2)}) collective-permute-start(bf16[32,4608]{1,0:T(8,128)(2,1)S(1)} %add_convert_fusion.13), channel_id=1, source_target_pairs={{0,8},{4,12},{8,0},{12,4},{16,24},{20,28},{24,16},{28,20},{1,9},{5... | collective-permute-start | bytes 884744 | tf_op jit(solution)/shard_map/ppermute | solution.py:35
  510.3 26.9 %collective-permute-start.26 = (bf16[192,2304]{1,0:T(8,128)(2,1)S(1)}, bf16[192,2304]{1,0:T(8,128)(2,1)S(1)}, u32[]{:S(2)}, u32[]{:S(2)}) collective-permute-start(bf16[192,2304]{1,0:T(8,128)(2,1)S(1)} %fusion.28), channel_id=1, source_target_pairs={{0,4},{4,0},{8,12},{12,8},{16,20},{20,16},{24,28},{28,24},{1,5},{5... | collective-permute-start | bytes 2654216 | tf_op jit(solution)/shard_map/ppermute | solution.py:35
  512.2 29.0 %collective-permute-start.42 = (bf16[768,768]{1,0:T(8,128)(2,1)S(1)}, bf16[768,768]{1,0:T(8,128)(2,1)S(1)}, u32[]{:S(2)}, u32[]{:S(2)}) collective-permute-start(bf16[768,768]{1,0:T(8,128)(2,1)S(1)} %add_convert_fusion.1), channel_id=1, source_target_pairs={{0,8},{4,12},{8,0},{12,4},{16,24},{20,28},{24,16},{28,20},{1,9},{5... | collective-permute-start | bytes 3538952 | tf_op jit(solution)/shard_map/ppermute | solution.py:35
  522.2 47.8 %collective-permute-start.37 = (bf16[192,3072]{1,0:T(8,128)(2,1)S(1)}, bf16[192,3072]{1,0:T(8,128)(2,1)S(1)}, u32[]{:S(2)}, u32[]{:S(2)}) collective-permute-start(bf16[192,3072]{1,0:T(8,128)(2,1)S(1)} %add_convert_fusion.4), channel_id=1, source_target_pairs={{0,8},{4,12},{8,0},{12,4},{16,24},{20,28},{24,16},{28,20},{1,9},{5... | collective-permute-start | bytes 3538952 | tf_op jit(solution)/shard_map/ppermute | solution.py:35
  523.1 69.4 %collective-permute-start.48 = (bf16[32,4608]{1,0:T(8,128)(2,1)S(1)}, bf16[32,4608]{1,0:T(8,128)(2,1)S(1)}, u32[]{:S(2)}, u32[]{:S(2)}) collective-permute-start(bf16[32,4608]{1,0:T(8,128)(2,1)S(1)} %add_convert_fusion.12), channel_id=1, source_target_pairs={{0,24},{4,28},{8,16},{12,20},{16,8},{20,12},{24,0},{28,4},{1,25},{... | collective-permute-start | bytes 884744 | tf_op jit(solution)/shard_map/ppermute | solution.py:35
  537.5 54.3 %collective-permute-start.27 = (bf16[192,2304]{1,0:T(8,128)(2,1)S(1)}, bf16[192,2304]{1,0:T(8,128)(2,1)S(1)}, u32[]{:S(2)}, u32[]{:S(2)}) collective-permute-start(bf16[192,2304]{1,0:T(8,128)(2,1)S(1)} %add_convert_fusion.7), channel_id=1, source_target_pairs={{0,8},{4,12},{8,0},{12,4},{16,24},{20,28},{24,16},{28,20},{1,9},{5... | collective-permute-start | bytes 2654216 | tf_op jit(solution)/shard_map/ppermute | solution.py:35
  541.5 144.6 %collective-permute-start.43 = (bf16[768,768]{1,0:T(8,128)(2,1)S(1)}, bf16[768,768]{1,0:T(8,128)(2,1)S(1)}, u32[]{:S(2)}, u32[]{:S(2)}) collective-permute-start(bf16[768,768]{1,0:T(8,128)(2,1)S(1)} %add_convert_fusion), channel_id=1, source_target_pairs={{0,24},{4,28},{8,16},{12,20},{16,8},{20,12},{24,0},{28,4},{1,25},{... | collective-permute-start | bytes 3538952 | tf_op jit(solution)/shard_map/ppermute | solution.py:35
  570.3 117.4 %collective-permute-start.38 = (bf16[192,3072]{1,0:T(8,128)(2,1)S(1)}, bf16[192,3072]{1,0:T(8,128)(2,1)S(1)}, u32[]{:S(2)}, u32[]{:S(2)}) collective-permute-start(bf16[192,3072]{1,0:T(8,128)(2,1)S(1)} %add_convert_fusion.3), channel_id=1, source_target_pairs={{0,24},{4,28},{8,16},{12,20},{16,8},{20,12},{24,0},{28,4},{1,25},{... | collective-permute-start | bytes 3538952 | tf_op jit(solution)/shard_map/ppermute | solution.py:35
  592.0 92.7 %collective-permute-start.28 = (bf16[192,2304]{1,0:T(8,128)(2,1)S(1)}, bf16[192,2304]{1,0:T(8,128)(2,1)S(1)}, u32[]{:S(2)}, u32[]{:S(2)}) collective-permute-start(bf16[192,2304]{1,0:T(8,128)(2,1)S(1)} %add_convert_fusion.6), channel_id=1, source_target_pairs={{0,24},{4,28},{8,16},{12,20},{16,8},{20,12},{24,0},{28,4},{1,25},{... | collective-permute-start | bytes 2654216 | tf_op jit(solution)/shard_map/ppermute | solution.py:35
  (47 other events, 221.4 us)
